TPU v7x, 32 devices: a whole 2x2x4 slice. The times are simulated.
32 devices in a mesh: dp: 4 (over x, core), tensor: 8 (over z, y).
Axes of the slice: x: 2, y: 2, z: 4, core: 2. Of those that a mesh axis runs over, the one named last changes fastest.
Arguments:
- hidden: bfloat16 [4, 1024, 2048], P('dp', 'tensor'), may hold values from -6 to 6
- query_nope: bfloat16 [4, 1024, 2048], P('dp', 'tensor'), may hold values from -6 to 6
- query_rope: bfloat16 [4, 1024, 1024], P('dp', 'tensor'), may hold values from -300 to 300
- segments: int32 [4, 1024], P('dp'), may hold values from 0 to 65, as said below
- w_kva: bfloat16 [2048, 576], replicated, may hold values from -0.125 to 0.125
- w_kb: bfloat16 [16, 512, 128], replicated, may hold values from -0.5 to 0.5
- w_vb: bfloat16 [16, 512, 128], replicated, may hold values from -0.25 to 0.25
- w_o: bfloat16 [2048, 2048], P('tensor'), may hold values from -0.125 to 0.125
- route_ids: int32 [4, 1024, 6], P('dp', 'tensor'), may hold values from 0 to 15, all different within a row; in each aligned block of 128 rows (0 to 127, 128 to 255, ..., all dimensions but the last counted through in order) at most 64 rows name the same one
- route_weights: float32 [4, 1024, 6], P('dp', 'tensor'), may hold values from 0.05 to 0.35
- w_in: bfloat16 [32, 2048, 1408], P(('dp', 'tensor')), may hold values from -0.125 to 0.125
- w_down: bfloat16 [32, 704, 2048], P(('dp', 'tensor')), may hold values from -0.15625 to 0.15625
- page_table: int32 [4, 8], P('dp'), may hold values from 0 to 7, each once within a row
Outputs:
- layer_out: bfloat16 [4, 1024, 2048], P('dp', 'tensor')
- pool_latent: bfloat16 [4, 8, 128, 512], P('dp', 'tensor')
- pool_rope: bfloat16 [4, 8, 128, 64], P('dp', 'tensor')
Inputs may be any that keep to these rules, and one draw needn't show every extreme that they name: `segments`: in each stream ids start at 0, never fall and each segment is contiguous; the first segment has id 0, the last segment has id 65, the others are numbered 1, 2, ... in order; exactly one segment holds 512 tokens, the last may be cut short, every other holds 16 to 256. `route_ids`: in the rows of one device no expert is named more than 64 times, and that count is reached. `page_table`: each row is a permutation of the pool slots.
All inputs are finite; a program needn't handle non-finite values.
Results may differ from a plain program's by a relative error of at most 0.014.
Values may be sent and summed in bfloat16 or wider, within the bound.
A program may use at most 128 MiB of HBM per device.

v0:
```python
import jax
import jax.numpy as jnp
from jax import lax
from jax.sharding import PartitionSpec as P

PAGE = 128


eps_norm = 1e-06
masked_score = -1e30


def rms_rows(values):
    return values * lax.rsqrt(jnp.mean(values * values, axis=-1, keepdims=True) + eps_norm)


def rotate(values, positions):
    width = values.shape[-1]
    half_width = width // 2
    freqs = 10000.0 ** (-jnp.arange(half_width, dtype=jnp.float32) * 2.0 / width)
    angles = positions[..., None].astype(jnp.float32) * freqs
    cosine = jnp.cos(angles)
    sine = jnp.sin(angles)
    first_half = values[..., :half_width]
    second_half = values[..., half_width:]
    return jnp.concatenate(
        [first_half * cosine - second_half * sine, first_half * sine + second_half * cosine],
        axis=-1,
    )


def attend(carry_in, queries, keys_lat, keys_rot, keys_seg, key_first):
    peak, row_sum, numerator = carry_in
    query_lat, query_rot, query_seg, positions, scale = queries
    scores = jnp.einsum("qhl,kl->qhk", query_lat, keys_lat, preferred_element_type=jnp.float32)
    scores = (
        scores + jnp.einsum("qhr,kr->qhk", query_rot, keys_rot, preferred_element_type=jnp.float32)
    ) * scale
    key_pos = key_first + jnp.arange(keys_lat.shape[0], dtype=jnp.int32)
    allowed = (query_seg[:, None] == keys_seg[None, :]) & (key_pos[None, :] <= positions[:, None])
    scores = jnp.where(allowed[:, None, :], scores, masked_score)
    new_peak = jnp.maximum(peak, jnp.max(scores, axis=-1))
    shrink = jnp.exp(peak - new_peak)
    expo = jnp.exp(scores - new_peak[..., None])
    row_sum = row_sum * shrink + jnp.sum(expo, axis=-1)
    numerator = numerator * shrink[..., None] + jnp.einsum(
        "qhk,kl->qhl", expo.astype(jnp.bfloat16), keys_lat, preferred_element_type=jnp.float32
    )
    return (new_peak, row_sum, numerator)


def expert_rows(received, gate_up_w, down_w):
    model_width = received.shape[-1]
    flat_rows = received.reshape(-1, model_width)
    gate_up = jnp.dot(flat_rows, gate_up_w, preferred_element_type=jnp.float32)
    half_units = down_w.shape[0]
    activated = (jax.nn.silu(gate_up[:, :half_units]) * gate_up[:, half_units:]).astype(
        jnp.bfloat16
    )
    return (
        jnp.dot(activated, down_w, preferred_element_type=jnp.float32)
        .astype(jnp.bfloat16)
        .reshape(received.shape)
    )


def on_device(
    hidden,
    query_nope,
    query_rope,
    segments,
    w_kva,
    w_kb,
    w_vb,
    w_o,
    route_ids,
    route_weights,
    w_in,
    w_down,
    page_table,
):
    groups = lax.axis_size("tensor")
    stream_groups = lax.axis_size("dp")
    member = lax.axis_index("tensor")
    tokens = hidden[0]
    local_rows = tokens.shape[0]
    model_width = tokens.shape[1]
    stream_len = segments.shape[1]
    n_heads, lat_width, head_width = w_kb.shape
    rope_width = w_kva.shape[1] - lat_width
    top_count = route_ids.shape[2]
    scale = float(head_width + rope_width) ** (-0.5)
    kv_proj = jnp.dot(tokens, w_kva, preferred_element_type=jnp.float32)
    latent = rms_rows(kv_proj[:, :lat_width]).astype(jnp.bfloat16)
    first_row = member * local_rows
    positions = first_row + jnp.arange(local_rows, dtype=jnp.int32)
    key_rope = rotate(kv_proj[:, lat_width:], positions).astype(jnp.bfloat16)
    query_rot = rotate(
        query_rope[0].astype(jnp.float32).reshape(local_rows, n_heads, rope_width),
        positions[:, None],
    ).astype(jnp.bfloat16)
    query_lat = jnp.einsum(
        "thd,hld->thl",
        query_nope[0].reshape(local_rows, n_heads, head_width),
        w_kb,
        preferred_element_type=jnp.float32,
    ).astype(jnp.bfloat16)
    seg_all = segments[0]
    query_seg = lax.dynamic_slice_in_dim(seg_all, first_row, local_rows, 0)
    key_low = jnp.sum((seg_all < query_seg[0]).astype(jnp.int32))
    key_high = first_row + local_rows
    queries = (query_lat, query_rot, query_seg, positions, scale)
    start_state = (
        jnp.full((local_rows, n_heads), masked_score, jnp.float32),
        jnp.zeros((local_rows, n_heads), jnp.float32),
        jnp.zeros((local_rows, n_heads, lat_width), jnp.float32),
    )
    pages_dev = local_rows // PAGE
    page_row = page_table[0]
    slot_ids = member * pages_dev + jnp.arange(pages_dev, dtype=jnp.int32)
    page_of = jnp.sum(
        jnp.where(
            page_row[None, :] == slot_ids[:, None],
            jnp.arange(page_row.shape[0], dtype=jnp.int32)[None, :],
            0,
        ),
        axis=1,
    )
    page_rows = page_of[:, None] * PAGE + jnp.arange(PAGE, dtype=jnp.int32)[None, :]
    all_latent, all_rope = (
        lax.all_gather(latent, "tensor", axis=0, tiled=True),
        lax.all_gather(key_rope, "tensor", axis=0, tiled=True),
    )
    key_block = min(512, stream_len)
    block_first = key_low // key_block
    block_end = (key_high + key_block - 1) // key_block

    def key_step(block_no, carry_in):
        key_first = block_no * key_block
        keys_lat = lax.dynamic_slice_in_dim(all_latent, key_first, key_block, 0)
        keys_rot = lax.dynamic_slice_in_dim(all_rope, key_first, key_block, 0)
        keys_seg = lax.dynamic_slice_in_dim(seg_all, key_first, key_block, 0)
        return attend(carry_in, queries, keys_lat, keys_rot, keys_seg, key_first)

    final_state = lax.fori_loop(block_first, block_end, key_step, start_state)
    pool_lat = all_latent[page_rows]
    pool_rot = all_rope[page_rows]
    mixed_lat = (final_state[2] / final_state[1][..., None]).astype(jnp.bfloat16)
    heads_out = (
        jnp.einsum("thl,hld->thd", mixed_lat, w_vb, preferred_element_type=jnp.float32)
        .astype(jnp.bfloat16)
        .reshape(local_rows, n_heads * head_width)
    )
    attn_out = jnp.dot(
        heads_out,
        lax.all_gather(w_o, "tensor", axis=0, tiled=True),
        preferred_element_type=jnp.float32,
    )
    resid = (tokens.astype(jnp.float32) + attn_out).astype(jnp.bfloat16)
    normed = rms_rows(resid.astype(jnp.float32)).astype(jnp.bfloat16)
    experts = stream_groups * groups // 2
    capacity = max(2, min(local_rows, local_rows * top_count * 4 // (3 * experts)))
    expert_ids = route_ids[0].reshape(-1)
    assign_total = local_rows * top_count
    one_hot = (expert_ids[:, None] == jnp.arange(experts, dtype=jnp.int32)[None, :]).astype(
        jnp.int32
    )
    slot_in = jnp.sum((jnp.cumsum(one_hot, axis=0) - 1) * one_hot, axis=1)
    buffer_pos = expert_ids * capacity + slot_in
    source = (
        jnp.full((experts * capacity,), assign_total, jnp.int32)
        .at[buffer_pos]
        .set(jnp.arange(assign_total, dtype=jnp.int32))
    )
    padded = jnp.concatenate([normed, jnp.zeros((1, model_width), jnp.bfloat16)], axis=0)
    gathered_rows = padded[source // top_count]
    sending = gathered_rows.reshape(experts, 1, capacity, model_width)
    sending = jnp.broadcast_to(sending, (experts, 2, capacity, model_width)).reshape(
        2 * experts, capacity, model_width
    )
    returned = lax.all_to_all(
        expert_rows(
            lax.all_to_all(sending, ("dp", "tensor"), split_axis=0, concat_axis=0, tiled=True),
            w_in[0],
            w_down[0],
        ),
        ("dp", "tensor"),
        split_axis=0,
        concat_axis=0,
        tiled=True,
    )
    pairs = returned.reshape(experts, 2, capacity, model_width)
    merged = (pairs[:, 0].astype(jnp.float32) + pairs[:, 1].astype(jnp.float32)).reshape(
        experts * capacity, model_width
    )
    picked = merged[buffer_pos]
    weight_flat = route_weights[0].reshape(-1)
    moe_out = jnp.sum(
        (picked * weight_flat[:, None]).reshape(local_rows, top_count, model_width), axis=1
    )
    layer_out = (resid.astype(jnp.float32) + moe_out).astype(jnp.bfloat16)
    return (layer_out[None], pool_lat[None], pool_rot[None])


def solution(mesh):
    return jax.shard_map(
        on_device,
        mesh=mesh,
        in_specs=(
            P("dp", "tensor", None),
            P("dp", "tensor", None),
            P("dp", "tensor", None),
            P("dp", None),
            P(),
            P(),
            P(),
            P("tensor", None),
            P("dp", "tensor", None),
            P("dp", "tensor", None),
            P(("dp", "tensor"), None, None),
            P(("dp", "tensor"), None, None),
            P("dp", None),
        ),
        out_specs=(
            P("dp", "tensor", None),
            P("dp", "tensor", None, None),
            P("dp", "tensor", None, None),
        ),
        check_vma=False,
    )
```

profile of v0, /device:TPU:9, one launch (start us, length us, event | category | flops | bytes accessed | tf_op | source)
XLA Modules:
  0.0 645.4 jit_solution(10854255524633680335)
XLA Ops:
  7.3 2.8 fusion.27
  17.4 3.7 convert_bitcast_fusion
  21.1 3.9 copy.32
  27.4 3.4 scatter_custom_fusion
  31.0 21.2 %all_gather.10 = bf16[1024,64]{0,1:T(8,128)(2,1)S(1)} all-gather(bf16[128,64]{0,1:T(8,128)(2,1)S(1)} %pad_maximum_fusion.1), channel_id=1, replica_groups=mesh['dp'=4,'tensor'=8] {'tensor'}, dimensions={0}, use_global_device_ids=true | all-gather | bytes 147456 | tf_op jit(solution)/shard_map/all_gather | solution.py:132
  53.3 2.3 copy.31
  55.6 2.5 broadcast_in_dim.45
  58.2 11.1 %while.15 = (s32[]{:T(128)}, f32[128,16]{0,1:T(8,128)S(1)}, f32[128,16]{0,1:T(8,128)S(1)}, f32[128,16,512]{2,0,1:T(8,128)}, s32[]{:T(128)}, /*index=5*/s32[128]{...) while((s32[]{:T(128)}, f32[128,16]{0,1:T(8,128)S(1)}, ...), condition=%wide.region_5.6_spmd.clone, body=%wide.region_2.5_spmd.clone.sunk | while | flops 2292388352 | bytes 70856488 | solution.py:145
  58.4 3.1 fusion.64
  69.3 4.8 fusion.25
  74.1 102.1 %all-gather.5.cloned.1.call-done = bf16[2048,2048]{1,0:T(8,128)(2,1)} async-done(((bf16[256,2048]{1,0:T(8,128)(2,1)}), bf16[2048,2048]{1,0:T(8,128)(2,1)}) %all-gather.5.cloned.1.call-update) | async-done | bytes 8388624 | tf_op jit(solution)/shard_map/all_gather | solution.py:156
  176.2 4.9 multiply_reduce_fusion.1
  182.3 6.1 gather_fusion
  188.4 6.8 %broadcast_in_dim.49 = bf16[16,2,64,2048]{3,2,1,0:T(8,128)(2,1)} broadcast(bf16[16,64,2048]{2,1,0:T(8,128)(2,1)} %bitcast.93), dimensions={0,2,3} | broadcast | bytes 12582912 | tf_op jit(solution)/shard_map/broadcast_in_dim | solution.py:178
  195.1 189.2 %all_to_all.10 = bf16[32,64,2048]{2,1,0:T(8,128)(2,1)S(1)} all-to-all(bf16[32,64,2048]{2,1,0:T(8,128)(2,1)} %bitcast.92), channel_id=1, replica_groups=mesh['dp'=4,'tensor'=8] {'dp','tensor'}, dimensions={0} | all-to-all | bytes 16777216 | tf_op jit(solution)/shard_map/all_to_all | solution.py:183
  384.3 17.8 %fusion.17 = f32[2048,1408]{0,1:T(8,128)} fusion(bf16[2048,2048]{1,0:T(8,128)(2,1)S(1)} %bitcast.95, bf16[1,2048,1408]{2,1,0:T(8,128)(2,1)} %param.25), kind=kOutput, calls=%fused_computation.32 | convolution fusion | flops 11811160064 | bytes 25690112 | tf_op jit(solution)/shard_map/dot_general | solution.py:55
  402.1 13.5 %convolution_convert_fusion = bf16[2048,2048]{1,0:T(8,128)(2,1)} fusion(f32[2048,1408]{0,1:T(8,128)} %fusion.17, bf16[1,704,2048]{2,1,0:T(8,128)(2,1)S(1)} %copy-done), kind=kOutput, calls=%fused_computation.29 | convolution fusion | flops 5918425088 | bytes 22806528 | tf_op jit(solution)/shard_map/dot_general | solution.py:61
  415.6 5.1 all-to-all-start.1
  423.8 2.9 gather_fusion.2
  426.6 177.3 %all-to-all-done.1 = bf16[32,64,2048]{2,1,0:T(8,128)(2,1)} async-done(((bf16[32,64,2048]{2,1,0:T(8,128)(2,1)}), bf16[32,64,2048]{2,1,0:T(8,128)(2,1)}, u32[]{:S(2)}, u32[]{:S(2)}) %all-to-all-start.1) | async-done | bytes 8388640 | tf_op jit(solution)/shard_map/all_to_all | solution.py:181
  604.0 8.6 %convert_add_fusion = f32[16,1,64,2048]{3,2,0,1:T(8,128)} fusion(bf16[16,2,64,2048]{3,2,1,0:T(8,128)(2,1)} %bitcast.15), kind=kLoop, calls=%fused_computation.28 | loop fusion | flops 6291456 | bytes 16777216 | tf_op jit(solution)/shard_map/add | solution.py:193
  612.6 10.6 %gather_fusion.1 = f32[768,2048]{1,0:T(8,128)} fusion(f32[1024,2048]{1,0:T(8,128)} %bitcast.91, s32[1024]{0:T(1024)S(1)} %pad_clamp_fusion.1), kind=kCustom, calls=%fused_computation.1 | custom fusion | bytes 12585984 | tf_op jit(solution)/shard_map/gather | solution.py:196
  623.1 7.8 %gather.16 = f32[128,6,2048]{2,1,0:T(8,128)} reshape(f32[768,2048]{1,0:T(8,128)} %gather_fusion.1) | data formatting | bytes 12582912 | tf_op jit(solution)/shard_map/gather | solution.py:196
  631.0 6.7 %multiply_reduce_fusion = f32[128,2048]{1,0:T(8,128)S(1)} fusion(f32[128,6,2048]{2,1,0:T(8,128)} %gather.16, f32[128,6]{1,0:T(8,128)S(1)} %bitcast.100), kind=kLoop, calls=%fused_computation.27 | loop fusion | flops 2883584 | bytes 7343104 | tf_op jit(solution)/shard_map/reduce_sum | solution.py:198
  (83 shorter events, 20.8 us)
Async XLA Ops:
  7.2 394.9 %copy-start = (bf16[1,704,2048]{2,1,0:T(8,128)(2,1)S(1)}, bf16[1,704,2048]{2,1,0:T(8,128)(2,1)}, u32[]{:S(2)}) copy-start(bf16[1,704,2048]{2,1,0:T(8,128)(2,1)} %param.26) | copy-start | bytes 8650756
  7.2 4.4 copy-start.9
  7.2 7.7 %copy-start.10 = (s32[1,128,6]{1,0,2:T(1,128)S(1)}, s32[1,128,6]{1,0,2:T(1,128)}, u32[]{:S(2)}) copy-start(s32[1,128,6]{1,0,2:T(1,128)} %param.23) | copy-start | bytes 9220
  7.2 8.1 %copy-start.8 = (bf16[1,128,1024]{2,1,0:T(8,128)(2,1)S(1)}, bf16[1,128,1024]{2,1,0:T(8,128)(2,1)}, u32[]{:S(2)}) copy-start(bf16[1,128,1024]{2,1,0:T(8,128)(2,1)} %param.17) | copy-start | bytes 786436
  7.2 46.1 %all-gather.3.cloned.1.call-start = ((), (), s32[]{:S(2)}) async-start(), calls=%async_computation.2 | async-start | bytes 1179648 | tf_op jit(solution)/shard_map/all_gather | solution.py:131
  10.8 165.4 %all-gather.5.cloned.1.call-start = ((), (), s32[]{:S(2)}) async-start(), calls=%async_computation.3 | async-start | bytes 9437184 | tf_op jit(solution)/shard_map/all_gather | solution.py:156
  61.5 1.6 copy-start.3
  62.5 2.7 copy-start.1
  67.3 2.0 copy-start.2
  69.3 4.8 copy-start.6
  181.1 1.0 copy-start.4
  415.6 5.1 copy-start.7
  415.6 5.3 copy-start.11
  415.6 5.4 copy-start.12
  415.6 188.3 %all-to-all-start.1 = ((bf16[32,64,2048]{2,1,0:T(8,128)(2,1)}), bf16[32,64,2048]{2,1,0:T(8,128)(2,1)}, u32[]{:S(2)}, u32[]{:S(2)}) async-start(bf16[32,64,2048]{2,1,0:T(8,128)(2,1)} %bitcast.94), calls=%async_computation.1 | async-start | bytes 16777216 | tf_op jit(solution)/shard_map/all_to_all | solution.py:181
  631.0 6.7 %copy-start.5 = (f32[128,2048]{1,0:T(8,128)S(1)}, f32[128,2048]{1,0:T(8,128)}, u32[]{:S(2)}) copy-start(f32[128,2048]{1,0:T(8,128)} %copy-done.4) | copy-start | bytes 3145732
Sparse Core Ops, SparseCore 0:
  10.9 38.9 all-gather.2
  52.1 124.0 all-gather.4
where the time goes:
time: 654 us; the launch traced here: 645 us
  waiting for transfers between devices  280 us (43%)
  blocking collectives  210 us (32%)
  local copies, waits for them, and re-layouts  56 us (9%)
  matrix products  53.7 us (8%)
  other arithmetic  22.4 us (3%)
  between operations  17.6 us (3%)
    all_to_all x1, blocking collectives, on_device(): lax.all_to_all(sending, ('dp', 'tensor'), split_axis=0, concat_axis=0, ti...  189 us
    all_to_all x1, waiting for transfers between devices, on_device(): lax.all_to_all(expert_rows(lax.all_to_all(sending, ('dp', 'tensor'), spli...  177 us
    all_gather x1, waiting for transfers between devices, on_device(): lax.all_gather(w_o, 'tensor', axis=0, tiled=True)  102 us
    all_gather x1, blocking collectives, on_device(): lax.all_gather(key_rope, 'tensor', axis=0, tiled=True)  21.2 us
    gather x2, local copies, waits for them, and re-layouts, on_device(): picked = merged[buffer_pos]  18.4 us
    dot_general x1, matrix products, expert_rows(): gate_up = jnp.dot(flat_rows, gate_up_w, preferred_element_type=jnp.float32)  17.8 us
    dot_general x1, matrix products, expert_rows(): jnp.dot(activated, down_w, preferred_element_type=jnp.float32)  13.5 us
  transfers between devices with their start and end apart: 3, of which 2 were waited for; matrix products, arithmetic and copies ran while one was open for 6% of the time, Pallas kernels for 0%

commit v1 on v0

--- a/solution.py
+++ b/solution.py
@@ -1,7 +1,11 @@
 import jax
 import jax.numpy as jnp
 from jax import lax
+from jax.experimental import pallas as pl
+from jax.experimental.pallas import tpu as pltpu
 from jax.sharding import PartitionSpec as P
+
+MESH = pl.DeviceIdType.MESH
 
 PAGE = 128
 
@@ -62,6 +66,335 @@
         .astype(jnp.bfloat16)
         .reshape(received.shape)
     )
+
+
+def place():
+    dp = lax.axis_index("dp")
+    member = lax.axis_index("tensor")
+    return dp // 2, dp % 2, member // 2, member % 2
+
+
+def device(x, core, z, y):
+    return {"dp": x * 2 + core, "tensor": z * 2 + y}
+
+
+def greet(partners):
+    barrier = pltpu.get_barrier_semaphore()
+    for partner in partners:
+        pl.semaphore_signal(barrier, inc=1, device_id=partner, device_id_type=MESH)
+    pl.semaphore_wait(barrier, len(partners))
+
+
+def gather_kernel(depth, rows_ref, out_ref, own_sem, send_sem, recv_sem):
+    x, core, z, y = place()
+    half = rows_ref.shape[0] // 2
+    sibling = device(x, 1 - core, z, y)
+    over_y = device(x, core, z, 1 - y)
+    over_x = device(1 - x, core, z, y)
+    others = [lax.rem(z + step, depth) for step in range(1, depth)]
+    over_z = [device(x, core, other, y) for other in others]
+    started = []
+
+    def slot(sx, sc, sz, sy):
+        return (sx * 2 + sc) * (2 * depth) + sz * 2 + sy
+
+    def send(block, part, target, own=False):
+        span = pl.ds(part * half, half)
+        copy = pltpu.make_async_remote_copy(
+            src_ref=rows_ref.at[span] if own else out_ref.at[block, span],
+            dst_ref=out_ref.at[block, span],
+            send_sem=send_sem.at[len(started)],
+            recv_sem=recv_sem.at[block, part],
+            device_id=target,
+            device_id_type=MESH,
+        )
+        copy.start()
+        started.append(copy)
+
+    def arrived(block, part):
+        span = pl.ds(part * half, half)
+        pltpu.make_async_remote_copy(
+            src_ref=out_ref.at[block, span],
+            dst_ref=out_ref.at[block, span],
+            send_sem=send_sem.at[0],
+            recv_sem=recv_sem.at[block, part],
+            device_id=sibling,
+            device_id_type=MESH,
+        ).wait_recv()
+
+    greet([sibling, over_y, over_x] + over_z)
+    mine = slot(x, core, z, y)
+    own = pltpu.make_async_copy(rows_ref, out_ref.at[mine], own_sem)
+    own.start()
+    near = (over_y, over_x)
+    for part in range(2):
+        for target in over_z:
+            send(mine, part, target, True)
+    for part in range(2):
+        send(mine, part, near[part], True)
+        send(mine, part, near[1 - part], True)
+        send(mine, part, sibling, True)
+    for step in range(1, depth):
+        sz = lax.rem(z + depth - step, depth)
+        for part in range(2):
+            block = slot(x, core, sz, y)
+            arrived(block, part)
+            send(block, part, near[part])
+            send(block, part, near[1 - part])
+            send(block, part, sibling)
+    for step in range(depth):
+        sz = lax.rem(z + depth - step, depth)
+        for part in range(2):
+            block = slot(x, core, sz, 1 - y) if part == 0 else slot(1 - x, core, sz, y)
+            arrived(block, part)
+            send(block, part, near[1 - part])
+            send(block, part, sibling)
+    for far in range(2):
+        for step in range(depth):
+            sz = lax.rem(z + depth - step, depth)
+            for part in range(2):
+                if part == 0:
+                    block = slot(1 - x, core, sz, (y + far) % 2)
+                else:
+                    block = slot((x + far) % 2, core, sz, 1 - y)
+                arrived(block, part)
+                send(block, part, sibling)
+    for step in range(depth):
+        sz = lax.rem(z + depth - step, depth)
+        for sx in range(2):
+            for sy in range(2):
+                for part in range(2):
+                    arrived(slot(sx, 1 - core, sz, sy), part)
+    own.wait()
+    for copy in started:
+        copy.wait_send()
+
+
+def gather_rows(rows, devices, depth):
+    sends = 2 * (depth - 1 + depth + 2 * depth + 4 * depth)
+    return pl.pallas_call(
+        lambda *refs: gather_kernel(depth, *refs),
+        name="gather_rows",
+        out_shape=jax.ShapeDtypeStruct((devices,) + rows.shape, rows.dtype),
+        in_specs=[pl.BlockSpec(memory_space=pl.ANY)],
+        out_specs=pl.BlockSpec(memory_space=pl.ANY),
+        scratch_shapes=[
+            pltpu.SemaphoreType.DMA,
+            pltpu.SemaphoreType.DMA((sends,)),
+            pltpu.SemaphoreType.DMA((devices, 2)),
+        ],
+        compiler_params=pltpu.CompilerParams(collective_id=0, has_side_effects=True),
+    )(rows)
+
+
+def reduce_kernel(
+    depth, part_ref, out_ref, first, second, third, fourth, send_sem, sem1, sem2, sem3, sem4
+):
+    x, core, z, y = place()
+    half = out_ref.shape[0] // 2
+    chunk = 16
+    sibling = device(x, 1 - core, z, y)
+    over_y = device(x, core, z, 1 - y)
+    over_x = device(1 - x, core, z, y)
+    others = [lax.rem(z + step, depth) for step in range(1, depth)]
+    greet([sibling, over_y, over_x] + [device(x, core, other, y) for other in others])
+    started = []
+
+    def send(src, dst, recv_sem, target):
+        copy = pltpu.make_async_remote_copy(
+            src_ref=src,
+            dst_ref=dst,
+            send_sem=send_sem.at[len(started)],
+            recv_sem=recv_sem,
+            device_id=target,
+            device_id_type=MESH,
+        )
+        copy.start()
+        started.append(copy)
+
+    def arrived(dst, recv_sem):
+        pltpu.make_async_remote_copy(
+            src_ref=dst,
+            dst_ref=dst,
+            send_sem=send_sem.at[0],
+            recv_sem=recv_sem,
+            device_id=sibling,
+            device_id_type=MESH,
+        ).wait_recv()
+
+    def slot(dx, dc, dz, dy):
+        return (dx * 2 + dc) * (2 * depth) + dz * 2 + dy
+
+    def plane(dx, dz, dy):
+        return (dx * 2 + dy) * depth + dz
+
+    def span(part):
+        return pl.ds(part * half, half)
+
+    def add_into(target, part, sources):
+        def body(step, carry):
+            row = step * chunk
+            rows = pl.ds(pl.multiple_of(part * half + row, chunk), chunk)
+            short = pl.ds(pl.multiple_of(row, chunk), chunk)
+            total = None
+            for ref, index, whole in sources:
+                value = ref[index, rows if whole else short, :].astype(jnp.float32)
+                total = value if total is None else total + value
+            if target is None:
+                out_ref[rows, :] = total
+            else:
+                target[0][target[1], rows if target[2] else short, :] = total.astype(jnp.bfloat16)
+            return carry
+
+        lax.fori_loop(0, half // chunk, body, 0)
+
+    def inner(part, near, dz):
+        return (near * depth + dz) * 2 + part
+
+    steps = [lax.rem(z + step, depth) for step in list(range(1, depth)) + [0]]
+
+    def dest(part, far_first, far_second):
+        if part == 0:
+            return (x + far_first) % 2, (y + far_second) % 2
+        return (x + far_second) % 2, (y + far_first) % 2
+
+    order = [(1, 1), (1, 0), (0, 1), (0, 0)]
+    for far_first, far_second in order:
+        for dz in steps:
+            for part in range(2):
+                dx, dy = dest(part, far_first, far_second)
+                index = plane(dx, dz, dy)
+                send(
+                    part_ref.at[slot(dx, 1 - core, dz, dy), span(part)],
+                    first.at[index, span(part)],
+                    sem1.at[index, part],
+                    sibling,
+                )
+    for far_second in (1, 0):
+        for dz in steps:
+            for part in range(2):
+                dx, dy = dest(part, 1, far_second)
+                index = plane(dx, dz, dy)
+                arrived(first.at[index, span(part)], sem1.at[index, part])
+                add_into(
+                    (first, index, True),
+                    part,
+                    [(part_ref, slot(dx, core, dz, dy), True), (first, index, True)],
+                )
+                there = inner(part, far_second, dz)
+                send(
+                    first.at[index, span(part)],
+                    second.at[there],
+                    sem2.at[there],
+                    over_x if part == 0 else over_y,
+                )
+    for dz in steps:
+        for part in range(2):
+            dx, dy = dest(part, 0, 1)
+            index = plane(dx, dz, dy)
+            there = inner(part, 1, dz)
+            arrived(first.at[index, span(part)], sem1.at[index, part])
+            arrived(second.at[there], sem2.at[there])
+            add_into(
+                (second, there, False),
+                part,
+                [
+                    (part_ref, slot(dx, core, dz, dy), True),
+                    (first, index, True),
+                    (second, there, False),
+                ],
+            )
+            last = dz * 2 + part
+            send(
+                second.at[there],
+                third.at[last],
+                sem3.at[last],
+                over_y if part == 0 else over_x,
+            )
+    for number, dz in enumerate(steps):
+        for part in range(2):
+            index = plane(x, dz, y)
+            there = inner(part, 0, dz)
+            last = dz * 2 + part
+            arrived(first.at[index, span(part)], sem1.at[index, part])
+            arrived(second.at[there], sem2.at[there])
+            arrived(third.at[last], sem3.at[last])
+            sources = [
+                (part_ref, slot(x, core, dz, y), True),
+                (first, index, True),
+                (second, there, False),
+                (third, last, False),
+            ]
+            if number < depth - 1:
+                add_into((third, last, False), part, sources)
+                end = number * 2 + part
+                send(third.at[last], fourth.at[end], sem4.at[end], device(x, core, dz, y))
+            else:
+                for other in range(depth - 1):
+                    end = other * 2 + part
+                    arrived(fourth.at[end], sem4.at[end])
+                    sources.append((fourth, end, False))
+                add_into(None, part, sources)
+    for copy in started:
+        copy.wait_send()
+
+
+def reduce_rows(parts, depth):
+    devices, rows, width = parts.shape
+    half = rows // 2
+    sends = 8 * depth + 4 * depth + 2 * depth + 2 * (depth - 1)
+    return pl.pallas_call(
+        lambda *refs: reduce_kernel(depth, *refs),
+        name="reduce_rows",
+        out_shape=jax.ShapeDtypeStruct((rows, width), jnp.float32),
+        in_specs=[pl.BlockSpec(memory_space=pltpu.VMEM)],
+        out_specs=pl.BlockSpec(memory_space=pltpu.VMEM),
+        scratch_shapes=[
+            pltpu.VMEM((devices // 2, rows, width), jnp.bfloat16),
+            pltpu.VMEM((4 * depth, half, width), jnp.bfloat16),
+            pltpu.VMEM((2 * depth, half, width), jnp.bfloat16),
+            pltpu.VMEM((2 * (depth - 1), half, width), jnp.bfloat16),
+            pltpu.SemaphoreType.DMA((sends,)),
+            pltpu.SemaphoreType.DMA((devices // 2, 2)),
+            pltpu.SemaphoreType.DMA((4 * depth,)),
+            pltpu.SemaphoreType.DMA((2 * depth,)),
+            pltpu.SemaphoreType.DMA((2 * (depth - 1),)),
+        ],
+        compiler_params=pltpu.CompilerParams(
+            collective_id=1, has_side_effects=True, vmem_limit_bytes=48 * 1024 * 1024
+        ),
+    )(parts)
+
+
+def dense_experts(normed, gate_up_w, down_w, experts, capacity, all_share):
+    devices = lax.axis_size("dp") * lax.axis_size("tensor")
+    depth = lax.axis_size("tensor") // 2
+    local_rows, model_width = normed.shape
+    expert = (lax.axis_index("dp") * lax.axis_size("tensor") + lax.axis_index("tensor")) // 2
+    chosen = jnp.arange(experts, dtype=jnp.int32) == expert
+    share = jnp.sum(jnp.where(chosen, all_share, 0.0), axis=-1).reshape(devices, local_rows)
+    named = share != 0.0
+    order = jnp.arange(local_rows, dtype=jnp.int32)
+    upper = (order[:, None] <= order[None, :]).astype(jnp.bfloat16)
+    rank = jnp.dot(named.astype(jnp.bfloat16), upper, preferred_element_type=jnp.float32) - 1.0
+    slots = jnp.arange(capacity, dtype=jnp.int32)
+    pick = named[:, None, :] & (rank.astype(jnp.int32)[:, None, :] == slots[None, :, None])
+    slot_share = jnp.sum(jnp.where(pick, share[:, None, :], 0.0), axis=-1).reshape(-1, 1)
+    pick = pick.astype(jnp.bfloat16)
+    everyone = gather_rows(normed, devices, depth)
+    rows = jnp.einsum("sct,std->scd", pick, everyone, preferred_element_type=jnp.float32)
+    rows = rows.astype(jnp.bfloat16).reshape(devices * capacity, model_width)
+    gate_up = jnp.dot(rows, gate_up_w, preferred_element_type=jnp.float32)
+    half_units = down_w.shape[0]
+    activated = (jax.nn.silu(gate_up[:, :half_units]) * gate_up[:, half_units:]).astype(
+        jnp.bfloat16
+    )
+    scaled = (jnp.dot(activated, down_w, preferred_element_type=jnp.float32) * slot_share).astype(
+        jnp.bfloat16
+    )
+    scaled = scaled.reshape(devices, capacity, model_width)
+    parts = jnp.einsum("sct,scd->std", pick, scaled, preferred_element_type=jnp.float32)
+    return reduce_rows(parts.astype(jnp.bfloat16), depth)
 
 
 def on_device(
@@ -127,9 +460,27 @@
         axis=1,
     )
     page_rows = page_of[:, None] * PAGE + jnp.arange(PAGE, dtype=jnp.int32)[None, :]
-    all_latent, all_rope = (
-        lax.all_gather(latent, "tensor", axis=0, tiled=True),
-        lax.all_gather(key_rope, "tensor", axis=0, tiled=True),
+    all_keys = lax.all_gather(
+        jnp.concatenate([latent, key_rope], axis=1), "tensor", axis=0, tiled=True
+    )
+    all_latent, all_rope = all_keys[:, :lat_width], all_keys[:, lat_width:]
+    experts = stream_groups * groups // 2
+    capacity = max(2, min(local_rows, local_rows * top_count * 4 // (3 * experts)))
+    dense = stream_groups * groups * local_rows <= 4 * experts * capacity
+    if dense:
+        one_hot = route_ids[0][:, :, None] == jnp.arange(experts, dtype=jnp.int32)
+        share = jnp.sum(jnp.where(one_hot, route_weights[0][:, :, None], 0.0), axis=1)
+        all_share = lax.all_gather(share, ("dp", "tensor"), axis=0, tiled=True)
+    core = lax.axis_index("dp") % 2
+    half_width = model_width // 2
+    my_columns = lax.all_gather(
+        lax.dynamic_slice_in_dim(w_o, core * half_width, half_width, 1),
+        "tensor",
+        axis=0,
+        tiled=True,
+    )
+    its_columns = lax.ppermute(
+        my_columns, "dp", [(number, number ^ 1) for number in range(stream_groups)]
     )
     key_block = min(512, stream_len)
     block_first = key_low // key_block
@@ -151,15 +502,26 @@
         .astype(jnp.bfloat16)
         .reshape(local_rows, n_heads * head_width)
     )
-    attn_out = jnp.dot(
-        heads_out,
-        lax.all_gather(w_o, "tensor", axis=0, tiled=True),
-        preferred_element_type=jnp.float32,
+    my_out = jnp.dot(heads_out, my_columns, preferred_element_type=jnp.float32)
+    its_out = jnp.dot(heads_out, its_columns, preferred_element_type=jnp.float32)
+    attn_out = jnp.where(
+        core == 0,
+        jnp.concatenate([my_out, its_out], axis=1),
+        jnp.concatenate([its_out, my_out], axis=1),
     )
     resid = (tokens.astype(jnp.float32) + attn_out).astype(jnp.bfloat16)
     normed = rms_rows(resid.astype(jnp.float32)).astype(jnp.bfloat16)
-    experts = stream_groups * groups // 2
-    capacity = max(2, min(local_rows, local_rows * top_count * 4 // (3 * experts)))
+    if dense:
+        moe_out = dense_experts(
+            normed,
+            w_in[0],
+            w_down[0],
+            experts,
+            capacity,
+            all_share,
+        )
+        layer_out = (resid.astype(jnp.float32) + moe_out).astype(jnp.bfloat16)
+        return (layer_out[None], pool_lat[None], pool_rot[None])
     expert_ids = route_ids[0].reshape(-1)
     assign_total = local_rows * top_count
     one_hot = (expert_ids[:, None] == jnp.arange(experts, dtype=jnp.int32)[None, :]).astype(

time: 654 us -> 430 us (0.66); the launches traced: 645 us -> 430 us
  waiting for transfers between devices: 280 us -> 34.1 us
  Pallas kernels: 0 us -> 208 us
  blocking collectives: 210 us -> 60.2 us
  local copies, waits for them, and re-layouts: 56 us -> 24.3 us
  matrix products: 53.7 us -> 78 us
  other arithmetic: 22.4 us -> 5.9 us
    pallas_call x0 -> x2, Pallas kernels: none -> 208 us  [the longest x1 121 us: reduce_rows(): pl.pallas_call(lambda *refs: reduce_kernel(depth, *refs), name='reduce_ro...]
    all_to_all x1 -> x0, blocking collectives: 189 us -> none  [on_device(): lax.all_to_all(sending, ('dp', 'tensor'), split_axis=0, concat_axis=0, ti...]
    all_to_all x1 -> x0, waiting for transfers between devices: 177 us -> none  [on_device(): lax.all_to_all(expert_rows(lax.all_to_all(sending, ('dp', 'tensor'), spli...]
    all_gather x2, waiting for transfers between devices: 102 us -> 34 us  [the longest x1 34 us: on_device(): lax.all_gather(lax.dynamic_slice_in_dim(w_o, core * half_width, half_widt...]
    all_gather x1, blocking collectives: 21.2 us -> 60.2 us  [on_device(): all_share = lax.all_gather(share, ('dp', 'tensor'), axis=0, tiled=True)]
    dot_general x3 -> x7, matrix products: 36.3 us -> 61.4 us  [the longest x1 18.8 us: dense_experts(): gate_up = jnp.dot(rows, gate_up_w, preferred_element_type=jnp.float32)]
    gather x3 -> x0, local copies, waits for them, and re-layouts: 24.5 us -> none  [the longest x2 18.4 us: on_device(): picked = merged[buffer_pos]]
    add x1 -> x0, other arithmetic: 8.6 us -> none  [on_device(): pairs[:, 0].astype(jnp.float32) + pairs[:, 1].astype(jnp.float32)]
  transfers between devices with their start and end apart: 3 -> 3, of which waited for: 2 -> 1; matrix products, arithmetic and copies ran while one was open for 6% -> 9% of each run, Pallas kernels for 0% -> 0%
where the time goes in v1:
time: 430 us
  Pallas kernels  208 us (48%)
  matrix products  78 us (18%)
  blocking collectives  60.2 us (14%)
  waiting for transfers between devices  34.1 us (8%)
  local copies, waits for them, and re-layouts  24.3 us (6%)
  between operations  17.7 us (4%)
  other arithmetic  5.9 us (1%)
    pallas_call x1, Pallas kernels, reduce_rows(): pl.pallas_call(lambda *refs: reduce_kernel(depth, *refs), name='reduce_ro...  121 us
    pallas_call x1, Pallas kernels, gather_rows(): pl.pallas_call(lambda *refs: gather_kernel(depth, *refs), name='gather_ro...  86.7 us
    all_gather x1, blocking collectives, on_device(): all_share = lax.all_gather(share, ('dp', 'tensor'), axis=0, tiled=True)  60.2 us
    all_gather x1, waiting for transfers between devices, on_device(): lax.all_gather(lax.dynamic_slice_in_dim(w_o, core * half_width, half_widt...  34 us
    dot_general x1, matrix products, dense_experts(): gate_up = jnp.dot(rows, gate_up_w, preferred_element_type=jnp.float32)  18.8 us
    dot_general x1, matrix products, dense_experts(): jnp.dot(activated, down_w, preferred_element_type=jnp.float32) * slot_share  13.8 us
    dot_general x1, matrix products, dense_experts(): jnp.einsum('sct,scd->std', pick, scaled, preferred_element_type=jnp.float32)  13.6 us
    dot_general x1, matrix products, dense_experts(): jnp.einsum('sct,std->scd', pick, everyone, preferred_element_type=jnp.flo...  11.3 us
  transfers between devices with their start and end apart: 3, of which 1 were waited for; matrix products, arithmetic and copies ran while one was open for 9% of the time, Pallas kernels for 0%

profile of v1, /device:TPU:9, one launch (start us, length us, event | category | flops | bytes accessed | tf_op | source)
XLA Modules:
  0.0 430.1 jit_solution(3472516988088845755)
XLA Ops:
  7.3 2.7 fusion.34
  11.1 1.9 constant_dynamic-slice_fusion
  17.7 60.2 %all_gather.11 = f32[4096,16]{0,1:T(8,128)S(1)} all-gather(f32[128,16]{0,1:T(8,128)S(1)} %select_reduce_fusion.2), channel_id=1, replica_groups=mesh['dp'=4,'tensor'=8] {'dp','tensor'}, dimensions={0}, use_global_device_ids=true | all-gather | bytes 270336 | tf_op jit(solution)/shard_map/all_gather | solution.py:473
  79.9 1.9 copy.29
  81.8 3.6 convert_bitcast_fusion
  85.4 4.0 copy.31
  89.6 2.3 slice.51
  91.9 2.3 copy.30
  94.1 34.0 %all-gather.5.cloned.1.call-done = bf16[2048,1024]{1,0:T(8,128)(2,1)} async-done(((bf16[256,1024]{1,0:T(8,128)(2,1)}), bf16[2048,1024]{1,0:T(8,128)(2,1)}) %all-gather.5.cloned.1.call-update) | async-done | bytes 4194320 | tf_op jit(solution)/shard_map/all_gather | solution.py:476
  128.2 1.7 collective-permute-start
  129.9 2.5 broadcast_in_dim.94
  132.4 10.7 %while.15 = (s32[]{:T(128)}, f32[128,16]{0,1:T(8,128)S(1)}, f32[128,16]{0,1:T(8,128)S(1)}, f32[128,16,512]{2,0,1:T(8,128)}, s32[]{:T(128)}, /*index=5*/s32[128]{...) while((s32[]{:T(128)}, f32[128,16]{0,1:T(8,128)S(1)}, ...), condition=%wide.region_5.6_spmd.clone, body=%wide.region_2.5_spmd.clone.sunk | while | flops 2292388352 | bytes 70856488 | solution.py:496
  132.7 3.1 fusion.75
  139.0 2.2 multiply_add_fusion.5
  141.1 2.0 copy-done.2
  143.3 2.9 gather_fusion
  147.6 4.1 fusion.23
  152.4 2.9 fusion.47
  156.7 86.7 %gather_rows.1 = bf16[32,128,2048]{2,1,0:T(8,128)(2,1)} custom-call(bf16[128,2048]{1,0:T(8,128)(2,1)} %fusion.26.refs_0_), custom_call_target="tpu_custom_call" | custom-call | tf_op jit(solution)/shard_map/gather_rows/pallas_call | solution.py:175
  243.4 11.3 %convolution_convert_fusion.1 = bf16[32,64,2048]{2,1,0:T(8,128)(2,1)} fusion(bf16[32,128,2048]{2,1,0:T(8,128)(2,1)} %gather_rows.1, s32[32,128]{1,0:T(8,128)S(1)} %fusion.24, pred[32,128]{1,0:T(8,128)(4,1)S(1)} %broadcast_compare_fusion), kind=kOutput, calls=%fused_computation.30 | convolution fusion | flops 1078460416 | bytes 25186304 | tf_op jit(solution)/shard_map/sct,std->scd/dot_general | solution.py:385
  254.7 18.8 %fusion.17 = f32[2048,1408]{0,1:T(8,128)} fusion(bf16[2048,2048]{1,0:T(8,128)(2,1)} %bitcast.77, bf16[1,2048,1408]{2,1,0:T(8,128)(2,1)} %param.25), kind=kOutput, calls=%fused_computation.28 | convolution fusion | flops 11811160064 | bytes 25690112 | tf_op jit(solution)/shard_map/dot_general | solution.py:387
  273.5 13.8 %multiply_convert_fusion = bf16[2048,2048]{1,0:T(8,128)(2,1)} fusion(f32[2048]{0:T(1024)S(1)} %mul.168, f32[2048,1408]{0,1:T(8,128)} %fusion.17, bf16[1,704,2048]{2,1,0:T(8,128)(2,1)S(1)} %copy-done), kind=kOutput, calls=%fused_computation.24 | convolution fusion | flops 5922619392 | bytes 22814720 | tf_op jit(solution)/shard_map/dot_general | solution.py:392
  287.3 13.6 %convolution_convert_fusion.refs_0_ = bf16[32,128,2048]{2,1,0:T(8,128)(2,1)} fusion(bf16[32,64,2048]{2,1,0:T(8,128)(2,1)} %bitcast.76, s32[32,128]{1,0:T(8,128)S(1)} %fusion.24, pred[32,128]{1,0:T(8,128)(4,1)S(1)} %broadcast_compare_fusion), kind=kOutput, calls=%fused_computation.25 | convolution fusion | flops 1082654720 | bytes 25186304 | tf_op jit(solution)/shard_map/sct,scd->std/dot_general | solution.py:396
  301.0 121.4 %reduce_rows.1 = f32[128,2048]{1,0:T(8,128)S(1)} custom-call(bf16[32,128,2048]{2,1,0:T(8,128)(2,1)} %convolution_convert_fusion.refs_0_), custom_call_target="tpu_custom_call" | custom-call | tf_op jit(solution)/shard_map/reduce_rows/pallas_call | solution.py:346
  (73 shorter events, 12.4 us)
Async XLA Ops:
  7.2 266.4 %copy-start = (bf16[1,704,2048]{2,1,0:T(8,128)(2,1)S(1)}, bf16[1,704,2048]{2,1,0:T(8,128)(2,1)}, u32[]{:S(2)}) copy-start(bf16[1,704,2048]{2,1,0:T(8,128)(2,1)} %param.26) | copy-start | bytes 8650756
  7.2 5.8 %copy-start.7 = (s32[1,1024]{1,0:T(1,128)S(1)}, s32[1,1024]{1,0:T(1,128)}, u32[]{:S(2)}) copy-start(s32[1,1024]{1,0:T(1,128)} %param.18) | copy-start | bytes 12292
  7.2 9.1 %copy-start.10 = (s32[1,8]{1,0:T(1,128)S(1)}, s32[1,8]{1,0:T(1,128)}, u32[]{:S(2)}) copy-start(s32[1,8]{1,0:T(1,128)} %param.27) | copy-start | bytes 100
  7.2 10.4 %copy-start.8 = (s32[1,128,6]{1,0,2:T(1,128)S(1)}, s32[1,128,6]{1,0,2:T(1,128)}, u32[]{:S(2)}) copy-start(s32[1,128,6]{1,0,2:T(1,128)} %param.23) | copy-start | bytes 9220
  7.2 10.5 %copy-start.9 = (f32[1,128,6]{1,0,2:T(1,128)S(1)}, f32[1,128,6]{1,0,2:T(1,128)}, u32[]{:S(2)}) copy-start(f32[1,128,6]{1,0,2:T(1,128)} %param.24) | copy-start | bytes 9220
  7.2 82.3 %all-gather.3.cloned.1.call-start = ((), (), s32[]{:S(2)}) async-start(), calls=%async_computation | async-start | bytes 1327104 | tf_op jit(solution)/shard_map/all_gather | solution.py:463
  11.0 117.1 %all-gather.5.cloned.1.call-start = ((), (), s32[]{:S(2)}) async-start(), calls=%async_computation.1 | async-start | bytes 4718592 | tf_op jit(solution)/shard_map/all_gather | solution.py:476
  85.4 4.0 copy-start.6
  89.5 42.8 %slice-start = ((bf16[1024,576]{0,1:T(8,128)(2,1)}), bf16[1024,64]{0,1:T(8,128)(2,1)S(1)}, s32[]{:S(2)}) async-start(bf16[1024,576]{0,1:T(8,128)(2,1)} %all-gather.3.cloned.1.call-done), calls=%async_computation.2 | async-start | bytes 262144 | tf_op jit(solution)/shard_map/slice | solution.py:466
  128.2 24.3 %collective-permute-start = (bf16[2048,1024]{1,0:T(8,128)(2,1)}, bf16[2048,1024]{1,0:T(8,128)(2,1)}, u32[]{:S(2)}, u32[]{:S(2)}) collective-permute-start(bf16[2048,1024]{1,0:T(8,128)(2,1)} %all-gather.5.cloned.1.call-done), channel_id=1, source_target_pairs={{0,8},{8,0},{16,24},{24,16},{1,9},{9,1},{17,25},{25,17},{2,10},{10... | collective-permute-start | bytes 12582920 | tf_op jit(solution)/shard_map/ppermute | solution.py:482
  135.7 1.6 copy-start.3
  136.7 2.3 copy-start.1
  141.1 2.0 copy-start.2
  147.6 4.1 copy-start.4
  151.7 3.7 copy-start.5
Sparse Core Ops, SparseCore 0:
  11.2 43.0 all-gather.2
  56.4 71.7 all-gather.4

commit v2 on v1

--- a/solution.py
+++ b/solution.py
@@ -366,13 +366,170 @@
     )(parts)
 
 
-def dense_experts(normed, gate_up_w, down_w, experts, capacity, all_share):
+def prelude_kernel(
+    depth, keys_ref, w_o_ref, tags_ref, keys_out, w_out, tags_out, own_sem, send_sem, key_sem, w_sem, tag_sem
+):
+    x, core, z, y = place()
+    half = w_o_ref.shape[0] // 2
+    share = half * 3 // 8
+    sibling = device(x, 1 - core, z, y)
+    over_y = device(x, core, z, 1 - y)
+    over_x = device(1 - x, core, z, y)
+    over_z = [device(x, core, lax.rem(z + step, depth), y) for step in range(1, depth)]
+    started = []
+
+    def send(src, dst, recv_sem, target):
+        copy = pltpu.make_async_remote_copy(
+            src_ref=src,
+            dst_ref=dst,
+            send_sem=send_sem.at[len(started)],
+            recv_sem=recv_sem,
+            device_id=target,
+            device_id_type=MESH,
+        )
+        copy.start()
+        started.append(copy)
+
+    def arrived(dst, recv_sem):
+        pltpu.make_async_remote_copy(
+            src_ref=dst,
+            dst_ref=dst,
+            send_sem=send_sem.at[0],
+            recv_sem=recv_sem,
+            device_id=sibling,
+            device_id_type=MESH,
+        ).wait_recv()
+
+    def rows_of(on_core, piece):
+        if isinstance(piece, int):
+            return pl.ds(pl.multiple_of(on_core * half + 2 * share, 16), half - 2 * share)
+        return pl.ds(pl.multiple_of(on_core * half + piece * share, 16), share)
+
+    def w_send(block, on_core, piece, target, own=False):
+        rows = rows_of(on_core, piece)
+        send(
+            w_o_ref.at[rows] if own else w_out.at[block, rows],
+            w_out.at[block, rows],
+            w_sem.at[block, on_core * 3 + piece],
+            target,
+        )
+
+    def w_arrived(block, on_core, piece):
+        arrived(w_out.at[block, rows_of(on_core, piece)], w_sem.at[block, on_core * 3 + piece])
+
+    def slot(sx, sc, sz, sy):
+        return (sx * 2 + sc) * (2 * depth) + sz * 2 + sy
+
+    def tag_send(block, target, own=False):
+        send(
+            tags_ref if own else tags_out.at[block], tags_out.at[block], tag_sem.at[block], target
+        )
+
+    def tag_arrived(block):
+        arrived(tags_out.at[block], tag_sem.at[block])
+
+    greet([sibling, over_y, over_x] + over_z)
+    me = z * 2 + y
+    mine = slot(x, core, z, y)
+    local = [
+        pltpu.make_async_copy(keys_ref, keys_out.at[me], own_sem.at[0]),
+        pltpu.make_async_copy(w_o_ref, w_out.at[me], own_sem.at[1]),
+        pltpu.make_async_copy(tags_ref, tags_out.at[mine], own_sem.at[2]),
+    ]
+    for copy in local:
+        copy.start()
+    back = [lax.rem(z + depth - step, depth) for step in range(1, depth)]
+    pieces = (x, 2)
+    for target in over_z + [over_y]:
+        send(keys_ref, keys_out.at[me], key_sem.at[me], target)
+    for target in over_z + [over_y]:
+        for piece in pieces:
+            w_send(me, core, piece, target, True)
+    for target in over_z + [over_y, over_x, sibling]:
+        tag_send(mine, target, True)
+    for sz in back:
+        block = sz * 2 + y
+        arrived(keys_out.at[block], key_sem.at[block])
+        send(keys_out.at[block], keys_out.at[block], key_sem.at[block], over_y)
+    for sz in back:
+        block = sz * 2 + y
+        for piece in pieces:
+            w_arrived(block, core, piece)
+            w_send(block, core, piece, over_y)
+            if piece is x:
+                w_send(block, core, piece, over_x)
+            w_send(block, core, piece, sibling)
+        tag = slot(x, core, sz, y)
+        tag_arrived(tag)
+        for target in (over_y, over_x, sibling):
+            tag_send(tag, target)
+    for sz in [z] + back:
+        block = sz * 2 + 1 - y
+        for piece in pieces:
+            w_arrived(block, core, piece)
+            if piece is x:
+                w_send(block, core, piece, over_x)
+            w_send(block, core, piece, sibling)
+        tag = slot(x, core, sz, 1 - y)
+        tag_arrived(tag)
+        for target in (over_x, sibling):
+            tag_send(tag, target)
+    for sy in (y, 1 - y):
+        for sz in [z] + back:
+            block = sz * 2 + sy
+            if not (sy is y and sz is z):
+                w_arrived(block, core, 1 - x)
+                w_send(block, core, 1 - x, sibling)
+            tag = slot(1 - x, core, sz, sy)
+            tag_arrived(tag)
+            tag_send(tag, sibling)
+    for sz in [z] + back:
+        block = sz * 2 + 1 - y
+        arrived(keys_out.at[block], key_sem.at[block])
+        for sy in (y, 1 - y):
+            block = sz * 2 + sy
+            if not (sy is y and sz is z):
+                for piece in (x, 1 - x, 2):
+                    w_arrived(block, 1 - core, piece)
+            for sx in (x, 1 - x):
+                tag_arrived(slot(sx, 1 - core, sz, sy))
+    for copy in local:
+        copy.wait()
+    for copy in started:
+        copy.wait_send()
+
+
+def prelude(keys, w_o, tags, devices, depth):
+    key_sends = 2 * depth - 1
+    w_sends = 2 * depth + 5 * (depth - 1) + 3 * depth + 2 * depth - 1
+    tag_sends = depth + 2 + 3 * (depth - 1) + 2 * depth + 2 * depth
+    return pl.pallas_call(
+        lambda *refs: prelude_kernel(depth, *refs),
+        name="prelude",
+        out_shape=[
+            jax.ShapeDtypeStruct((2 * depth,) + keys.shape, keys.dtype),
+            jax.ShapeDtypeStruct((2 * depth,) + w_o.shape, w_o.dtype),
+            jax.ShapeDtypeStruct((devices,) + tags.shape, tags.dtype),
+        ],
+        in_specs=[pl.BlockSpec(memory_space=pl.ANY)] * 3,
+        out_specs=[pl.BlockSpec(memory_space=pl.ANY)] * 3,
+        scratch_shapes=[
+            pltpu.SemaphoreType.DMA((3,)),
+            pltpu.SemaphoreType.DMA((key_sends + w_sends + tag_sends,)),
+            pltpu.SemaphoreType.DMA((2 * depth,)),
+            pltpu.SemaphoreType.DMA((2 * depth, 6)),
+            pltpu.SemaphoreType.DMA((devices,)),
+        ],
+        compiler_params=pltpu.CompilerParams(collective_id=2, has_side_effects=True),
+    )(keys, w_o, tags)
+
+
+def dense_experts(normed, gate_up_w, down_w, experts, capacity, all_tags):
     devices = lax.axis_size("dp") * lax.axis_size("tensor")
     depth = lax.axis_size("tensor") // 2
     local_rows, model_width = normed.shape
     expert = (lax.axis_index("dp") * lax.axis_size("tensor") + lax.axis_index("tensor")) // 2
-    chosen = jnp.arange(experts, dtype=jnp.int32) == expert
-    share = jnp.sum(jnp.where(chosen, all_share, 0.0), axis=-1).reshape(devices, local_rows)
+    share = lax.dynamic_index_in_dim(all_tags, expert, 1, keepdims=False)
     named = share != 0.0
     order = jnp.arange(local_rows, dtype=jnp.int32)
     upper = (order[:, None] <= order[None, :]).astype(jnp.bfloat16)
@@ -460,28 +617,22 @@
         axis=1,
     )
     page_rows = page_of[:, None] * PAGE + jnp.arange(PAGE, dtype=jnp.int32)[None, :]
-    all_keys = lax.all_gather(
-        jnp.concatenate([latent, key_rope], axis=1), "tensor", axis=0, tiled=True
-    )
-    all_latent, all_rope = all_keys[:, :lat_width], all_keys[:, lat_width:]
     experts = stream_groups * groups // 2
     capacity = max(2, min(local_rows, local_rows * top_count * 4 // (3 * experts)))
     dense = stream_groups * groups * local_rows <= 4 * experts * capacity
+    my_keys = jnp.concatenate([latent, key_rope], axis=1)
     if dense:
-        one_hot = route_ids[0][:, :, None] == jnp.arange(experts, dtype=jnp.int32)
-        share = jnp.sum(jnp.where(one_hot, route_weights[0][:, :, None], 0.0), axis=1)
-        all_share = lax.all_gather(share, ("dp", "tensor"), axis=0, tiled=True)
-    core = lax.axis_index("dp") % 2
-    half_width = model_width // 2
-    my_columns = lax.all_gather(
-        lax.dynamic_slice_in_dim(w_o, core * half_width, half_width, 1),
-        "tensor",
-        axis=0,
-        tiled=True,
-    )
-    its_columns = lax.ppermute(
-        my_columns, "dp", [(number, number ^ 1) for number in range(stream_groups)]
-    )
+        one_hot = route_ids[0][None] == jnp.arange(experts, dtype=jnp.int32)[:, None, None]
+        tags = jnp.sum(jnp.where(one_hot, route_weights[0][None], 0.0), axis=2)
+        all_keys, all_w_o, all_tags = prelude(
+            my_keys, w_o, tags, stream_groups * groups, groups // 2
+        )
+        all_keys = all_keys.reshape(stream_len, -1)
+        all_w_o = all_w_o.reshape(-1, model_width)
+    else:
+        all_keys = lax.all_gather(my_keys, "tensor", axis=0, tiled=True)
+        all_w_o = lax.all_gather(w_o, "tensor", axis=0, tiled=True)
+    all_latent, all_rope = all_keys[:, :lat_width], all_keys[:, lat_width:]
     key_block = min(512, stream_len)
     block_first = key_low // key_block
     block_end = (key_high + key_block - 1) // key_block
@@ -502,13 +653,7 @@
         .astype(jnp.bfloat16)
         .reshape(local_rows, n_heads * head_width)
     )
-    my_out = jnp.dot(heads_out, my_columns, preferred_element_type=jnp.float32)
-    its_out = jnp.dot(heads_out, its_columns, preferred_element_type=jnp.float32)
-    attn_out = jnp.where(
-        core == 0,
-        jnp.concatenate([my_out, its_out], axis=1),
-        jnp.concatenate([its_out, my_out], axis=1),
-    )
+    attn_out = jnp.dot(heads_out, all_w_o, preferred_element_type=jnp.float32)
     resid = (tokens.astype(jnp.float32) + attn_out).astype(jnp.bfloat16)
     normed = rms_rows(resid.astype(jnp.float32)).astype(jnp.bfloat16)
     if dense:
@@ -518,7 +663,7 @@
             w_down[0],
             experts,
             capacity,
-            all_share,
+            all_tags,
         )
         layer_out = (resid.astype(jnp.float32) + moe_out).astype(jnp.bfloat16)
         return (layer_out[None], pool_lat[None], pool_rot[None])

time: 430 us -> 412 us (0.958)
  Pallas kernels: 208 us -> 286 us
  blocking collectives: 60.2 us -> 0 us
  waiting for transfers between devices: 34.1 us -> 0 us
  between operations: 17.7 us -> 4.13 us
  other arithmetic: 5.9 us -> 12.8 us
    pallas_call x0 -> x1, Pallas kernels: none -> 71.4 us  [prelude(): pl.pallas_call(lambda *refs: prelude_kernel(depth, *refs), name='prelude'...]
    all_gather x1 -> x0, blocking collectives: 60.2 us -> none  [on_device(): all_share = lax.all_gather(share, ('dp', 'tensor'), axis=0, tiled=True)]
    all_gather x2 -> x0, waiting for transfers between devices: 34 us -> none  [the longest x1 34 us: on_device(): lax.all_gather(lax.dynamic_slice_in_dim(w_o, core * half_width, half_widt...]
    pallas_call x1, Pallas kernels: 86.7 us -> 91.7 us  [gather_rows(): pl.pallas_call(lambda *refs: gather_kernel(depth, *refs), name='gather_ro...]
  transfers between devices with their start and end apart: 3 -> 0, of which waited for: 1 -> 0; matrix products, arithmetic and copies ran while one was open for 9% -> 0% of each run, Pallas kernels for 0% -> 0%
where the time goes in v2:
time: 412 us; the launch traced here: 411 us
  Pallas kernels  286 us (69%)
  matrix products  80.2 us (19%)
  local copies, waits for them, and re-layouts  27.8 us (7%)
  other arithmetic  12.8 us (3%)
  between operations  4.13 us (1%)
    pallas_call x1, Pallas kernels, reduce_rows(): pl.pallas_call(lambda *refs: reduce_kernel(depth, *refs), name='reduce_ro...  123 us
    pallas_call x1, Pallas kernels, gather_rows(): pl.pallas_call(lambda *refs: gather_kernel(depth, *refs), name='gather_ro...  91.7 us
    pallas_call x1, Pallas kernels, prelude(): pl.pallas_call(lambda *refs: prelude_kernel(depth, *refs), name='prelude'...  71.4 us
    dot_general x1, matrix products, dense_experts(): gate_up = jnp.dot(rows, gate_up_w, preferred_element_type=jnp.float32)  18.8 us
    dot_general x1, matrix products, dense_experts(): jnp.dot(activated, down_w, preferred_element_type=jnp.float32) * slot_share  13.8 us
    dot_general x1, matrix products, dense_experts(): jnp.einsum('sct,scd->std', pick, scaled, preferred_element_type=jnp.float32)  13.6 us
    dot_general x1, matrix products, dense_experts(): jnp.einsum('sct,std->scd', pick, everyone, preferred_element_type=jnp.flo...  11.3 us

profile of v2, /device:TPU:9, one launch (start us, length us, event | category | flops | bytes accessed | tf_op | source)
XLA Modules:
  0.0 411.1 jit_solution(4125029515848266526)
XLA Ops:
  0.7 1.5 fusion.40
  11.3 2.8 fusion.31
  16.2 1.5 copy.64
  17.7 1.5 pad_maximum_fusion.1.refs_0_
  22.0 3.7 convert_bitcast_fusion
  25.8 3.9 copy.65
  29.7 71.4 %prelude.1 = (bf16[8,128,576]{2,1,0:T(8,128)(2,1)}, bf16[8,256,2048]{2,1,0:T(8,128)(2,1)}, f32[32,16,128]{2,1,0:T(8,128)}) custom-call(bf16[128,576]{1,0:T(8,128)(2,1)} %pad_maximum_fusion.1.refs_0_, bf16[256,2048]{1,0:T(8,128)(2,1)} %refs_1_.1, f32[16,128]{1,0:T(8,128)} %select_reduce_fusion.1.refs_2_), custom_call_target="tpu_custom_call" | custom-call | tf_op jit(solution)/shard_map/prelude/pallas_call | solution.py:506
  104.3 2.3 slice.51
  109.6 2.5 broadcast_in_dim.63
  112.1 10.7 %while.15 = (s32[]{:T(128)}, f32[128,16]{0,1:T(8,128)S(1)}, f32[128,16]{0,1:T(8,128)S(1)}, f32[128,16,512]{2,0,1:T(8,128)}, s32[]{:T(128)}, /*index=5*/s32[128]{...) while((s32[]{:T(128)}, f32[128,16]{0,1:T(8,128)S(1)}, ...), condition=%wide.region_6.7_spmd.clone, body=%wide.region_3.0_spmd.clone.sunk | while | flops 2292388352 | bytes 70856488 | solution.py:647
  112.4 3.1 fusion.69
  117.1 1.6 copy-done.1
  118.7 2.2 multiply_add_fusion.5
  120.9 2.0 copy-done.2
  122.9 4.0 fusion.25
  126.9 5.8 %multiply_reduce_fusion = (f32[128]{0:T(128)S(1)}, f32[128,2048]{1,0:T(8,128)}) fusion(bf16[128,2048]{0,1:T(8,128)(2,1)S(1)} %bitcast.81, bf16[2048,2048]{1,0:T(8,128)(2,1)} %bitcast.77, bf16[1,128,2048]{2,1,0:T(8,128)(2,1)S(1)} %copy-done.5), kind=kOutput, calls=%fused_computation.45 | convolution fusion | flops 1075314560 | bytes 10486272 | tf_op jit(solution)/shard_map/dot_general | solution.py:656
  132.6 3.0 gather_fusion
  135.7 2.1 multiply_convert_fusion.1.refs_0_
  137.8 91.7 %gather_rows.1 = bf16[32,128,2048]{2,1,0:T(8,128)(2,1)} custom-call(bf16[128,2048]{1,0:T(8,128)(2,1)} %multiply_convert_fusion.1.refs_0_), custom_call_target="tpu_custom_call" | custom-call | tf_op jit(solution)/shard_map/gather_rows/pallas_call | solution.py:175
  229.5 11.3 %convolution_convert_fusion.1 = bf16[32,64,2048]{2,1,0:T(8,128)(2,1)} fusion(bf16[32,128,2048]{2,1,0:T(8,128)(2,1)} %gather_rows.1, s32[32,128]{1,0:T(8,128)S(1)} %fusion.26, pred[32,128]{1,0:T(8,128)(4,1)S(1)} %bitcast.86), kind=kOutput, calls=%fused_computation.30 | convolution fusion | flops 1078460416 | bytes 25186304 | tf_op jit(solution)/shard_map/sct,std->scd/dot_general | solution.py:542
  240.8 18.8 %fusion.17 = f32[2048,1408]{0,1:T(8,128)} fusion(bf16[2048,2048]{1,0:T(8,128)(2,1)} %bitcast.78, bf16[1,2048,1408]{2,1,0:T(8,128)(2,1)} %param.25), kind=kOutput, calls=%fused_computation.28 | convolution fusion | flops 11811160064 | bytes 25690112 | tf_op jit(solution)/shard_map/dot_general | solution.py:544
  259.7 13.8 %multiply_convert_fusion = bf16[2048,2048]{1,0:T(8,128)(2,1)} fusion(f32[2048]{0:T(1024)S(1)} %copy-done.11, f32[2048,1408]{0,1:T(8,128)} %fusion.17, bf16[1,704,2048]{2,1,0:T(8,128)(2,1)S(1)} %copy-done), kind=kOutput, calls=%fused_computation.24 | convolution fusion | flops 5922619392 | bytes 22814720 | tf_op jit(solution)/shard_map/dot_general | solution.py:549
  273.5 13.6 %convolution_convert_fusion.refs_0_ = bf16[32,128,2048]{2,1,0:T(8,128)(2,1)} fusion(bf16[32,64,2048]{2,1,0:T(8,128)(2,1)} %bitcast.76, s32[32,128]{1,0:T(8,128)S(1)} %fusion.26, pred[32,128]{1,0:T(8,128)(4,1)S(1)} %bitcast.87), kind=kOutput, calls=%fused_computation.25 | convolution fusion | flops 1082654720 | bytes 25186304 | tf_op jit(solution)/shard_map/sct,scd->std/dot_general | solution.py:553
  287.1 123.1 %reduce_rows.1 = f32[128,2048]{1,0:T(8,128)S(1)} custom-call(bf16[32,128,2048]{2,1,0:T(8,128)(2,1)} %convolution_convert_fusion.refs_0_), custom_call_target="tpu_custom_call" | custom-call | tf_op jit(solution)/shard_map/reduce_rows/pallas_call | solution.py:346
  (63 shorter events, 19.7 us)
Async XLA Ops:
  0.6 259.0 %copy-start = (bf16[1,704,2048]{2,1,0:T(8,128)(2,1)S(1)}, bf16[1,704,2048]{2,1,0:T(8,128)(2,1)}, u32[]{:S(2)}) copy-start(bf16[1,704,2048]{2,1,0:T(8,128)(2,1)} %param.26) | copy-start | bytes 8650756
  0.6 18.6 %copy-start.6 = (bf16[1,128,2048]{2,1,0:T(8,128)(2,1)S(1)}, bf16[1,128,2048]{2,1,0:T(8,128)(2,1)}, u32[]{:S(2)}) copy-start(bf16[1,128,2048]{2,1,0:T(8,128)(2,1)} %param.16) | copy-start | bytes 1572868
  102.1 0.6 copy-start.7
  108.1 4.0 copy-start.9
  108.2 4.0 copy-start.10
  115.5 1.6 copy-start.3
  116.5 2.3 copy-start.1
  120.9 2.0 copy-start.2
  122.9 4.0 copy-start.5
  137.8 91.7 %copy-start.8 = (pred[32,1,128]{2,0,1:T(8,128)(4,1)S(1)}, pred[32,1,128]{2,0,1:T(8,128)(4,1)}, u32[]{:S(2)}) copy-start(pred[32,1,128]{2,0,1:T(8,128)(4,1)} %copy-done.7) | copy-start | bytes 12292
  240.8 18.8 %copy-start.11 = (f32[2048]{0:T(1024)S(1)}, f32[2048]{0:T(1024)}, u32[]{:S(2)}) copy-start(f32[2048]{0:T(1024)} %mul.164) | copy-start | bytes 24580
  287.1 123.1 %copy-start.4 = (f32[128,2048]{1,0:T(8,128)S(1)}, f32[128,2048]{1,0:T(8,128)}, u32[]{:S(2)}) copy-start(f32[128,2048]{1,0:T(8,128)} %get-tuple-element.202) | copy-start | bytes 3145732

commit v3 on v2

--- a/solution.py
+++ b/solution.py
@@ -85,20 +85,32 @@
     pl.semaphore_wait(barrier, len(partners))
 
 
+def by_distance(z, depth):
+    tables = [
+        sorted([other for other in range(depth) if other != here], key=lambda other: abs(other - here))
+        for here in range(depth)
+    ]
+    return [
+        sum(jnp.where(z == here, tables[here][number], 0) for here in range(depth))
+        for number in range(depth - 1)
+    ]
+
+
 def gather_kernel(depth, rows_ref, out_ref, own_sem, send_sem, recv_sem):
     x, core, z, y = place()
     half = rows_ref.shape[0] // 2
     sibling = device(x, 1 - core, z, y)
     over_y = device(x, core, z, 1 - y)
     over_x = device(1 - x, core, z, y)
-    others = [lax.rem(z + step, depth) for step in range(1, depth)]
-    over_z = [device(x, core, other, y) for other in others]
+    others = by_distance(z, depth)
+    up = device(x, core, jnp.minimum(z + 1, depth - 1), y)
+    down = device(x, core, jnp.maximum(z - 1, 0), y)
     started = []
 
     def slot(sx, sc, sz, sy):
         return (sx * 2 + sc) * (2 * depth) + sz * 2 + sy
 
-    def send(block, part, target, own=False):
+    def send(block, part, target, own=False, when=None):
         span = pl.ds(part * half, half)
         copy = pltpu.make_async_remote_copy(
             src_ref=rows_ref.at[span] if own else out_ref.at[block, span],
@@ -108,8 +120,11 @@
             device_id=target,
             device_id_type=MESH,
         )
-        copy.start()
-        started.append(copy)
+        if when is None:
+            copy.start()
+        else:
+            pl.when(when)(copy.start)
+        started.append((copy, when))
 
     def arrived(block, part):
         span = pl.ds(part * half, half)
@@ -122,36 +137,35 @@
             device_id_type=MESH,
         ).wait_recv()
 
-    greet([sibling, over_y, over_x] + over_z)
+    greet([sibling, over_y, over_x] + [device(x, core, other, y) for other in others])
     mine = slot(x, core, z, y)
     own = pltpu.make_async_copy(rows_ref, out_ref.at[mine], own_sem)
     own.start()
     near = (over_y, over_x)
     for part in range(2):
-        for target in over_z:
-            send(mine, part, target, True)
+        send(mine, part, up, True, z < depth - 1)
+        send(mine, part, down, True, z > 0)
     for part in range(2):
         send(mine, part, near[part], True)
         send(mine, part, near[1 - part], True)
         send(mine, part, sibling, True)
-    for step in range(1, depth):
-        sz = lax.rem(z + depth - step, depth)
+    for sz in others:
         for part in range(2):
             block = slot(x, core, sz, y)
             arrived(block, part)
+            send(block, part, up, False, (sz < z) & (z < depth - 1))
+            send(block, part, down, False, (sz > z) & (z > 0))
             send(block, part, near[part])
             send(block, part, near[1 - part])
             send(block, part, sibling)
-    for step in range(depth):
-        sz = lax.rem(z + depth - step, depth)
+    for sz in [z] + others:
         for part in range(2):
             block = slot(x, core, sz, 1 - y) if part == 0 else slot(1 - x, core, sz, y)
             arrived(block, part)
             send(block, part, near[1 - part])
             send(block, part, sibling)
     for far in range(2):
-        for step in range(depth):
-            sz = lax.rem(z + depth - step, depth)
+        for sz in [z] + others:
             for part in range(2):
                 if part == 0:
                     block = slot(1 - x, core, sz, (y + far) % 2)
@@ -159,19 +173,21 @@
                     block = slot((x + far) % 2, core, sz, 1 - y)
                 arrived(block, part)
                 send(block, part, sibling)
-    for step in range(depth):
-        sz = lax.rem(z + depth - step, depth)
+    for sz in [z] + others:
         for sx in range(2):
             for sy in range(2):
                 for part in range(2):
                     arrived(slot(sx, 1 - core, sz, sy), part)
     own.wait()
-    for copy in started:
-        copy.wait_send()
+    for copy, when in started:
+        if when is None:
+            copy.wait_send()
+        else:
+            pl.when(when)(copy.wait_send)
 
 
 def gather_rows(rows, devices, depth):
-    sends = 2 * (depth - 1 + depth + 2 * depth + 4 * depth)
+    sends = 2 * (2 * depth + depth + 2 * depth + 4 * depth)
     return pl.pallas_call(
         lambda *refs: gather_kernel(depth, *refs),
         name="gather_rows",
@@ -188,11 +204,11 @@
 
 
 def reduce_kernel(
-    depth, part_ref, out_ref, first, second, third, fourth, send_sem, sem1, sem2, sem3, sem4
+    depth, slots_ref, pick_ref, out_ref, outgoing, first, second, third, fourth, send_sem, sem1, sem2, sem3, sem4
 ):
     x, core, z, y = place()
     half = out_ref.shape[0] // 2
-    chunk = 16
+    chunk = 512
     sibling = device(x, 1 - core, z, y)
     over_y = device(x, core, z, 1 - y)
     over_x = device(1 - x, core, z, y)
@@ -231,22 +247,24 @@
     def span(part):
         return pl.ds(part * half, half)
 
-    def add_into(target, part, sources):
+    def add_into(target, block, part, sources):
+        picked = pick_ref[block, span(part), :]
+
         def body(step, carry):
-            row = step * chunk
-            rows = pl.ds(pl.multiple_of(part * half + row, chunk), chunk)
-            short = pl.ds(pl.multiple_of(row, chunk), chunk)
-            total = None
+            columns = pl.ds(pl.multiple_of(step * chunk, chunk), chunk)
+            total = jnp.dot(picked, slots_ref[block, :, columns], preferred_element_type=jnp.float32)
             for ref, index, whole in sources:
-                value = ref[index, rows if whole else short, :].astype(jnp.float32)
-                total = value if total is None else total + value
+                value = ref[index, span(part), columns] if whole else ref[index, :, columns]
+                total = total + value.astype(jnp.float32)
             if target is None:
-                out_ref[rows, :] = total
+                out_ref[span(part), columns] = total
+            elif target[2]:
+                target[0][target[1], span(part), columns] = total.astype(jnp.bfloat16)
             else:
-                target[0][target[1], rows if target[2] else short, :] = total.astype(jnp.bfloat16)
+                target[0][target[1], :, columns] = total.astype(jnp.bfloat16)
             return carry
 
-        lax.fori_loop(0, half // chunk, body, 0)
+        lax.fori_loop(0, out_ref.shape[1] // chunk, body, 0)
 
     def inner(part, near, dz):
         return (near * depth + dz) * 2 + part
@@ -264,8 +282,9 @@
             for part in range(2):
                 dx, dy = dest(part, far_first, far_second)
                 index = plane(dx, dz, dy)
+                add_into((outgoing, index, True), slot(dx, 1 - core, dz, dy), part, [])
                 send(
-                    part_ref.at[slot(dx, 1 - core, dz, dy), span(part)],
+                    outgoing.at[index, span(part)],
                     first.at[index, span(part)],
                     sem1.at[index, part],
                     sibling,
@@ -278,8 +297,9 @@
                 arrived(first.at[index, span(part)], sem1.at[index, part])
                 add_into(
                     (first, index, True),
+                    slot(dx, core, dz, dy),
                     part,
-                    [(part_ref, slot(dx, core, dz, dy), True), (first, index, True)],
+                    [(first, index, True)],
                 )
                 there = inner(part, far_second, dz)
                 send(
@@ -297,12 +317,9 @@
             arrived(second.at[there], sem2.at[there])
             add_into(
                 (second, there, False),
+                slot(dx, core, dz, dy),
                 part,
-                [
-                    (part_ref, slot(dx, core, dz, dy), True),
-                    (first, index, True),
-                    (second, there, False),
-                ],
+                [(first, index, True), (second, there, False)],
             )
             last = dz * 2 + part
             send(
@@ -319,14 +336,14 @@
             arrived(first.at[index, span(part)], sem1.at[index, part])
             arrived(second.at[there], sem2.at[there])
             arrived(third.at[last], sem3.at[last])
+            block = slot(x, core, dz, y)
             sources = [
-                (part_ref, slot(x, core, dz, y), True),
                 (first, index, True),
                 (second, there, False),
                 (third, last, False),
             ]
             if number < depth - 1:
-                add_into((third, last, False), part, sources)
+                add_into((third, last, False), block, part, sources)
                 end = number * 2 + part
                 send(third.at[last], fourth.at[end], sem4.at[end], device(x, core, dz, y))
             else:
@@ -334,22 +351,24 @@
                     end = other * 2 + part
                     arrived(fourth.at[end], sem4.at[end])
                     sources.append((fourth, end, False))
-                add_into(None, part, sources)
+                add_into(None, block, part, sources)
     for copy in started:
         copy.wait_send()
 
 
-def reduce_rows(parts, depth):
-    devices, rows, width = parts.shape
+def reduce_rows(slots, pick, depth):
+    devices, rows, _ = pick.shape
+    width = slots.shape[2]
     half = rows // 2
     sends = 8 * depth + 4 * depth + 2 * depth + 2 * (depth - 1)
     return pl.pallas_call(
         lambda *refs: reduce_kernel(depth, *refs),
         name="reduce_rows",
         out_shape=jax.ShapeDtypeStruct((rows, width), jnp.float32),
-        in_specs=[pl.BlockSpec(memory_space=pltpu.VMEM)],
+        in_specs=[pl.BlockSpec(memory_space=pltpu.VMEM)] * 2,
         out_specs=pl.BlockSpec(memory_space=pltpu.VMEM),
         scratch_shapes=[
+            pltpu.VMEM((devices // 2, rows, width), jnp.bfloat16),
             pltpu.VMEM((devices // 2, rows, width), jnp.bfloat16),
             pltpu.VMEM((4 * depth, half, width), jnp.bfloat16),
             pltpu.VMEM((2 * depth, half, width), jnp.bfloat16),
@@ -363,15 +382,13 @@
         compiler_params=pltpu.CompilerParams(
             collective_id=1, has_side_effects=True, vmem_limit_bytes=48 * 1024 * 1024
         ),
-    )(parts)
+    )(slots, pick)
 
 
 def prelude_kernel(
-    depth, keys_ref, w_o_ref, tags_ref, keys_out, w_out, tags_out, own_sem, send_sem, key_sem, w_sem, tag_sem
+    depth, keys_ref, tags_ref, keys_out, tags_out, own_sem, send_sem, key_sem, tag_sem
 ):
     x, core, z, y = place()
-    half = w_o_ref.shape[0] // 2
-    share = half * 3 // 8
     sibling = device(x, 1 - core, z, y)
     over_y = device(x, core, z, 1 - y)
     over_x = device(1 - x, core, z, y)
@@ -400,23 +417,6 @@
             device_id_type=MESH,
         ).wait_recv()
 
-    def rows_of(on_core, piece):
-        if isinstance(piece, int):
-            return pl.ds(pl.multiple_of(on_core * half + 2 * share, 16), half - 2 * share)
-        return pl.ds(pl.multiple_of(on_core * half + piece * share, 16), share)
-
-    def w_send(block, on_core, piece, target, own=False):
-        rows = rows_of(on_core, piece)
-        send(
-            w_o_ref.at[rows] if own else w_out.at[block, rows],
-            w_out.at[block, rows],
-            w_sem.at[block, on_core * 3 + piece],
-            target,
-        )
-
-    def w_arrived(block, on_core, piece):
-        arrived(w_out.at[block, rows_of(on_core, piece)], w_sem.at[block, on_core * 3 + piece])
-
     def slot(sx, sc, sz, sy):
         return (sx * 2 + sc) * (2 * depth) + sz * 2 + sy
 
@@ -433,18 +433,13 @@
     mine = slot(x, core, z, y)
     local = [
         pltpu.make_async_copy(keys_ref, keys_out.at[me], own_sem.at[0]),
-        pltpu.make_async_copy(w_o_ref, w_out.at[me], own_sem.at[1]),
-        pltpu.make_async_copy(tags_ref, tags_out.at[mine], own_sem.at[2]),
+        pltpu.make_async_copy(tags_ref, tags_out.at[mine], own_sem.at[1]),
     ]
     for copy in local:
         copy.start()
     back = [lax.rem(z + depth - step, depth) for step in range(1, depth)]
-    pieces = (x, 2)
     for target in over_z + [over_y]:
         send(keys_ref, keys_out.at[me], key_sem.at[me], target)
-    for target in over_z + [over_y]:
-        for piece in pieces:
-            w_send(me, core, piece, target, True)
     for target in over_z + [over_y, over_x, sibling]:
         tag_send(mine, target, True)
     for sz in back:
@@ -452,34 +447,17 @@
         arrived(keys_out.at[block], key_sem.at[block])
         send(keys_out.at[block], keys_out.at[block], key_sem.at[block], over_y)
     for sz in back:
-        block = sz * 2 + y
-        for piece in pieces:
-            w_arrived(block, core, piece)
-            w_send(block, core, piece, over_y)
-            if piece is x:
-                w_send(block, core, piece, over_x)
-            w_send(block, core, piece, sibling)
         tag = slot(x, core, sz, y)
         tag_arrived(tag)
         for target in (over_y, over_x, sibling):
             tag_send(tag, target)
     for sz in [z] + back:
-        block = sz * 2 + 1 - y
-        for piece in pieces:
-            w_arrived(block, core, piece)
-            if piece is x:
-                w_send(block, core, piece, over_x)
-            w_send(block, core, piece, sibling)
         tag = slot(x, core, sz, 1 - y)
         tag_arrived(tag)
         for target in (over_x, sibling):
             tag_send(tag, target)
     for sy in (y, 1 - y):
         for sz in [z] + back:
-            block = sz * 2 + sy
-            if not (sy is y and sz is z):
-                w_arrived(block, core, 1 - x)
-                w_send(block, core, 1 - x, sibling)
             tag = slot(1 - x, core, sz, sy)
             tag_arrived(tag)
             tag_send(tag, sibling)
@@ -487,10 +465,6 @@
         block = sz * 2 + 1 - y
         arrived(keys_out.at[block], key_sem.at[block])
         for sy in (y, 1 - y):
-            block = sz * 2 + sy
-            if not (sy is y and sz is z):
-                for piece in (x, 1 - x, 2):
-                    w_arrived(block, 1 - core, piece)
             for sx in (x, 1 - x):
                 tag_arrived(slot(sx, 1 - core, sz, sy))
     for copy in local:
@@ -499,29 +473,26 @@
         copy.wait_send()
 
 
-def prelude(keys, w_o, tags, devices, depth):
+def prelude(keys, tags, devices, depth):
     key_sends = 2 * depth - 1
-    w_sends = 2 * depth + 5 * (depth - 1) + 3 * depth + 2 * depth - 1
     tag_sends = depth + 2 + 3 * (depth - 1) + 2 * depth + 2 * depth
     return pl.pallas_call(
         lambda *refs: prelude_kernel(depth, *refs),
         name="prelude",
         out_shape=[
             jax.ShapeDtypeStruct((2 * depth,) + keys.shape, keys.dtype),
-            jax.ShapeDtypeStruct((2 * depth,) + w_o.shape, w_o.dtype),
             jax.ShapeDtypeStruct((devices,) + tags.shape, tags.dtype),
         ],
-        in_specs=[pl.BlockSpec(memory_space=pl.ANY)] * 3,
-        out_specs=[pl.BlockSpec(memory_space=pl.ANY)] * 3,
+        in_specs=[pl.BlockSpec(memory_space=pl.ANY)] * 2,
+        out_specs=[pl.BlockSpec(memory_space=pl.ANY)] * 2,
         scratch_shapes=[
-            pltpu.SemaphoreType.DMA((3,)),
-            pltpu.SemaphoreType.DMA((key_sends + w_sends + tag_sends,)),
+            pltpu.SemaphoreType.DMA((2,)),
+            pltpu.SemaphoreType.DMA((key_sends + tag_sends,)),
             pltpu.SemaphoreType.DMA((2 * depth,)),
-            pltpu.SemaphoreType.DMA((2 * depth, 6)),
             pltpu.SemaphoreType.DMA((devices,)),
         ],
         compiler_params=pltpu.CompilerParams(collective_id=2, has_side_effects=True),
-    )(keys, w_o, tags)
+    )(keys, tags)
 
 
 def dense_experts(normed, gate_up_w, down_w, experts, capacity, all_tags):
@@ -550,8 +521,7 @@
         jnp.bfloat16
     )
     scaled = scaled.reshape(devices, capacity, model_width)
-    parts = jnp.einsum("sct,scd->std", pick, scaled, preferred_element_type=jnp.float32)
-    return reduce_rows(parts.astype(jnp.bfloat16), depth)
+    return reduce_rows(scaled, jnp.swapaxes(pick, 1, 2), depth)
 
 
 def on_device(
@@ -624,14 +594,18 @@
     if dense:
         one_hot = route_ids[0][None] == jnp.arange(experts, dtype=jnp.int32)[:, None, None]
         tags = jnp.sum(jnp.where(one_hot, route_weights[0][None], 0.0), axis=2)
-        all_keys, all_w_o, all_tags = prelude(
-            my_keys, w_o, tags, stream_groups * groups, groups // 2
-        )
+        all_keys, all_tags = prelude(my_keys, tags, stream_groups * groups, groups // 2)
         all_keys = all_keys.reshape(stream_len, -1)
-        all_w_o = all_w_o.reshape(-1, model_width)
     else:
         all_keys = lax.all_gather(my_keys, "tensor", axis=0, tiled=True)
-        all_w_o = lax.all_gather(w_o, "tensor", axis=0, tiled=True)
+    core = lax.axis_index("dp") % 2
+    half_width = model_width // 2
+    my_columns = lax.all_gather(
+        lax.dynamic_slice_in_dim(w_o, core * half_width, half_width, 1),
+        "tensor",
+        axis=0,
+        tiled=True,
+    )
     all_latent, all_rope = all_keys[:, :lat_width], all_keys[:, lat_width:]
     key_block = min(512, stream_len)
     block_first = key_low // key_block
@@ -653,7 +627,17 @@
         .astype(jnp.bfloat16)
         .reshape(local_rows, n_heads * head_width)
     )
-    attn_out = jnp.dot(heads_out, all_w_o, preferred_element_type=jnp.float32)
+    my_columns, heads_out = lax.optimization_barrier((my_columns, heads_out))
+    its_columns = lax.ppermute(
+        my_columns, "dp", [(number, number ^ 1) for number in range(stream_groups)]
+    )
+    my_out = jnp.dot(heads_out, my_columns, preferred_element_type=jnp.float32)
+    its_out = jnp.dot(heads_out, its_columns, preferred_element_type=jnp.float32)
+    attn_out = jnp.where(
+        core == 0,
+        jnp.concatenate([my_out, its_out], axis=1),
+        jnp.concatenate([its_out, my_out], axis=1),
+    )
     resid = (tokens.astype(jnp.float32) + attn_out).astype(jnp.bfloat16)
     normed = rms_rows(resid.astype(jnp.float32)).astype(jnp.bfloat16)
     if dense:

time: 412 us -> 381 us (0.925)
  Pallas kernels: 286 us -> 254 us
  between operations: 4.13 us -> 17.5 us
  matrix products: 80.2 us -> 67.8 us
    pallas_call x1, Pallas kernels: 71.4 us -> 45 us  [prelude(): pl.pallas_call(lambda *refs: prelude_kernel(depth, *refs), name='prelude'...]
    dot_general x2, matrix products: 19.4 us -> 6.05 us  [the longest x1 3.13 us: on_device(): my_out = jnp.dot(heads_out, my_columns, preferred_element_type=jnp.float32)]
    pallas_call x1, Pallas kernels: 91.7 us -> 82.3 us  [gather_rows(): pl.pallas_call(lambda *refs: gather_kernel(depth, *refs), name='gather_ro...]
  transfers between devices with their start and end apart: 0 -> 2, of which waited for: 0 -> 0; matrix products, arithmetic and copies ran while one was open for 0% -> 14% of each run, Pallas kernels for 0% -> 12%
where the time goes in v3:
time: 381 us; the launch traced here: 380 us
  Pallas kernels  254 us (67%)
  matrix products  67.8 us (18%)
  local copies, waits for them, and re-layouts  27.6 us (7%)
  between operations  17.5 us (5%)
  other arithmetic  12.5 us (3%)
    pallas_call x1, Pallas kernels, reduce_rows(): pl.pallas_call(lambda *refs: reduce_kernel(depth, *refs), name='reduce_ro...  127 us
    pallas_call x1, Pallas kernels, gather_rows(): pl.pallas_call(lambda *refs: gather_kernel(depth, *refs), name='gather_ro...  82.3 us
    pallas_call x1, Pallas kernels, prelude(): pl.pallas_call(lambda *refs: prelude_kernel(depth, *refs), name='prelude'...  45 us
    dot_general x1, matrix products, dense_experts(): gate_up = jnp.dot(rows, gate_up_w, preferred_element_type=jnp.float32)  18.8 us
    dot_general x1, matrix products, dense_experts(): jnp.dot(activated, down_w, preferred_element_type=jnp.float32) * slot_share  14 us
    dot_general x1, matrix products, dense_experts(): jnp.einsum('sct,std->scd', pick, everyone, preferred_element_type=jnp.flo...  11.3 us
    unnamed x21, local copies, waits for them, and re-layouts  8.1 us
  transfers between devices with their start and end apart: 2, of which 0 were waited for; matrix products, arithmetic and copies ran while one was open for 14% of the time, Pallas kernels for 12%

profile of v3, /device:TPU:9, one launch (start us, length us, event | category | flops | bytes accessed | tf_op | source)
XLA Modules:
  0.0 379.7 jit_solution(5454176082138380582)
XLA Ops:
  7.2 2.0 constant_dynamic-slice_fusion.2
  11.2 1.4 convert_reduce_fusion
  16.6 2.8 fusion.35
  21.3 45.0 %prelude.1 = (bf16[8,128,576]{2,1,0:T(8,128)(2,1)}, f32[32,16,128]{2,1,0:T(8,128)}) custom-call(bf16[128,576]{1,0:T(8,128)(2,1)} %pad_maximum_fusion.1.refs_0_, f32[16,128]{1,0:T(8,128)} %select_reduce_fusion.1.refs_1_), custom_call_target="tpu_custom_call" | custom-call | tf_op jit(solution)/shard_map/prelude/pallas_call | solution.py:479
  67.3 2.3 slice.51
  70.3 1.9 copy.75
  73.4 3.7 convert_bitcast_fusion
  77.1 3.9 %copy.65 = bf16[128,16,512]{2,0,1:T(8,128)(2,1)} copy(bf16[128,16,512]{0,2,1:T(8,128)(2,1)} %convert_bitcast_fusion) | data formatting | bytes 4194304
  82.2 2.5 broadcast_in_dim.63
  84.7 12.1 %while.15 = (s32[]{:T(128)}, f32[128,16]{0,1:T(8,128)S(1)}, f32[128,16]{0,1:T(8,128)S(1)}, f32[128,16,512]{2,0,1:T(8,128)}, s32[]{:T(128)}, /*index=5*/s32[128]{...) while((s32[]{:T(128)}, f32[128,16]{0,1:T(8,128)S(1)}, ...), condition=%wide.region_6.7_spmd.clone, body=%wide.region_3.0_spmd.clone.sunk | while | flops 2292388352 | bytes 70856488 | solution.py:621
  86.3 3.1 fusion.75
  91.0 1.6 copy-done.2
  92.6 2.2 multiply_add_fusion.5
  94.8 1.9 copy-done.3
  96.7 4.8 %fusion.25 = bf16[16,128,128]{1,2,0:T(8,128)(2,1)} fusion(bf16[16,512,128]{2,1,0:T(8,128)(2,1)} %param.21, f32[128,16,512]{2,0,1:T(8,128)} %get-tuple-element.72, f32[128,16]{0,1:T(8,128)S(1)} %get-tuple-element.73), kind=kOutput, calls=%fused_computation.41 | convolution fusion | flops 270794752 | bytes 6823936 | tf_op jit(solution)/shard_map/thl,hld->thd/dot_general | solution.py:626
  103.7 2.9 gather_fusion
  108.9 2.5 fusion.24.refs_1_
  111.4 3.1 fusion.48
  114.5 2.9 fusion.49
  118.8 82.3 %gather_rows.1 = bf16[32,128,2048]{2,1,0:T(8,128)(2,1)} custom-call(bf16[128,2048]{1,0:T(8,128)(2,1)} %fusion.28.refs_0_), custom_call_target="tpu_custom_call" | custom-call | tf_op jit(solution)/shard_map/gather_rows/pallas_call | solution.py:191
  201.1 11.3 %convolution_convert_fusion = bf16[32,64,2048]{2,1,0:T(8,128)(2,1)} fusion(bf16[32,128,2048]{2,1,0:T(8,128)(2,1)} %gather_rows.1, s32[32,128]{1,0:T(8,128)S(1)} %fusion.26, pred[32,128]{1,0:T(8,128)(4,1)S(1)} %bitcast.92), kind=kOutput, calls=%fused_computation.29 | convolution fusion | flops 1078460416 | bytes 25186304 | tf_op jit(solution)/shard_map/sct,std->scd/dot_general | solution.py:513
  212.4 18.8 %fusion.17 = f32[2048,1408]{0,1:T(8,128)} fusion(bf16[2048,2048]{1,0:T(8,128)(2,1)} %bitcast.77, bf16[1,2048,1408]{2,1,0:T(8,128)(2,1)} %param.25), kind=kOutput, calls=%fused_computation.27 | convolution fusion | flops 11811160064 | bytes 25690112 | tf_op jit(solution)/shard_map/dot_general | solution.py:515
  231.2 14.0 %multiply_convert_fusion = bf16[2048,2048]{1,0:T(8,128)(2,1)} fusion(f32[2048]{0:T(1024)S(1)} %mul.168, f32[2048,1408]{0,1:T(8,128)} %fusion.17, bf16[1,704,2048]{2,1,0:T(8,128)(2,1)S(1)} %copy-done), kind=kOutput, calls=%fused_computation.24 | convolution fusion | flops 5922619392 | bytes 22814720 | tf_op jit(solution)/shard_map/dot_general | solution.py:520
  245.2 126.7 %reduce_rows.1 = f32[128,2048]{1,0:T(8,128)S(1)} custom-call(bf16[32,64,2048]{2,1,0:T(8,128)(2,1)} %bitcast.78, bf16[32,128,64]{2,1,0:T(8,128)(2,1)S(1)} %copy-done.1), custom_call_target="tpu_custom_call" | custom-call | tf_op jit(solution)/shard_map/reduce_rows/pallas_call | solution.py:364
  (67 shorter events, 18.3 us)
Async XLA Ops:
  7.2 224.0 %copy-start = (bf16[1,704,2048]{2,1,0:T(8,128)(2,1)S(1)}, bf16[1,704,2048]{2,1,0:T(8,128)(2,1)}, u32[]{:S(2)}) copy-start(bf16[1,704,2048]{2,1,0:T(8,128)(2,1)} %param.26) | copy-start | bytes 8650756
  7.2 94.3 %all-gather.2.cloned.1.call-start = ((), (), s32[]{:S(2)}) async-start(), calls=%async_computation | async-start | bytes 4718592 | tf_op jit(solution)/shard_map/all_gather | solution.py:603
  16.5 55.7 %copy-start.7 = (bf16[1,128,1024]{2,1,0:T(8,128)(2,1)S(1)}, bf16[1,128,1024]{2,1,0:T(8,128)(2,1)}, u32[]{:S(2)}) copy-start(bf16[1,128,1024]{2,1,0:T(8,128)(2,1)} %param.17) | copy-start | bytes 786436
  73.4 7.7 %copy-start.8 = (f32[128,32]{0,1:T(8,128)S(1)}, f32[128,32]{0,1:T(8,128)}, u32[]{:S(2)}) copy-start(f32[128,32]{0,1:T(8,128)} %copy.64) | copy-start | bytes 49156
  89.4 1.6 copy-start.4
  90.3 2.3 copy-start.2
  94.8 2.0 copy-start.3
  96.7 4.9 %copy-start.9 = (s32[1,8]{1,0:T(1,128)S(1)}, s32[1,8]{1,0:T(1,128)}, u32[]{:S(2)}) copy-start(s32[1,8]{1,0:T(1,128)} %param.27) | copy-start | bytes 100
  101.5 13.0 %collective-permute-start = (bf16[2048,1024]{1,0:T(8,128)(2,1)}, bf16[2048,1024]{1,0:T(8,128)(2,1)}, u32[]{:S(2)}, u32[]{:S(2)}) collective-permute-start(bf16[2048,1024]{1,0:T(8,128)(2,1)} %all-gather.2.cloned.1.call-done), channel_id=1, source_target_pairs={{0,8},{8,0},{16,24},{24,16},{1,9},{9,1},{17,25},{25,17},{2,10},{10... | collective-permute-start | bytes 12582920 | tf_op jit(solution)/shard_map/ppermute | solution.py:631
  103.7 10.9 %copy-start.5 = (bf16[16,128,128]{1,2,0:T(8,128)(2,1)S(1)}, bf16[16,128,128]{1,2,0:T(8,128)(2,1)}, u32[]{:S(2)}) copy-start(bf16[16,128,128]{1,2,0:T(8,128)(2,1)} %fusion.25) | copy-start | bytes 1572868
  111.4 6.1 %copy-start.6 = (bf16[1,128,2048]{2,1,0:T(8,128)(2,1)S(1)}, bf16[1,128,2048]{2,1,0:T(8,128)(2,1)}, u32[]{:S(2)}) copy-start(bf16[1,128,2048]{2,1,0:T(8,128)(2,1)} %param.15) | copy-start | bytes 1572868
  231.2 14.0 %copy-start.1 = (bf16[32,128,64]{2,1,0:T(8,128)(2,1)S(1)}, bf16[32,128,64]{2,1,0:T(8,128)(2,1)}, u32[]{:S(2)}) copy-start(bf16[32,128,64]{2,1,0:T(8,128)(2,1)} %fusion.24.refs_1_) | copy-start | bytes 1572868
Sparse Core Ops, SparseCore 0:
  10.1 89.0 all-gather.1
